TPU v7x, 512 devices: a whole 4x8x8 slice. The times are simulated.
512 devices in a mesh: dp: 16 (over z, core), tensor: 32 (over x, y).
Axes of the slice: x: 4, y: 8, z: 8, core: 2. Of those that a mesh axis runs over, the one named last changes fastest.
Arguments:
- q_rows: bfloat16 [1024, 4096], P('dp', 'tensor'), parts along dimension 0, may hold values from -160 to 160, as said below
- k_cache: bfloat16 [64, 8192, 512], P('dp', 'tensor'), parts along dimension 0, may hold values from -6 to 6
- v_cache: bfloat16 [64, 8192, 512], P('dp', 'tensor'), parts along dimension 0, may hold values from -24 to 24
- k_tree: bfloat16 [64, 16, 512], P('dp'), parts along dimension 0, may hold values from -18 to 18
- v_tree: bfloat16 [64, 16, 512], P('dp'), parts along dimension 0, may hold values from -24 to 24
- residual: bfloat16 [1024, 8192], P('dp', 'tensor'), parts along dimension 0, may hold values from -2 to 2
- wo_rows: bfloat16 [4096, 8192], P('tensor'), may hold values from -1 to 1
- gain: bfloat16 [8192], P('tensor'), may hold values from 0.099609375 to 1.8984375
- parents: int32 [64, 16], P('dp'), parts along dimension 0, may hold values from 0 to 6, as said below
- cache_len: int32 [64], P('dp'), parts along dimension 0, may hold values from 1024 to 8192, as said below
- accepted_node: int32 [64], P('dp'), parts along dimension 0, may hold values from 0 to 15, as said below
Outputs:
- layer_out: bfloat16 [1024, 8192], P('dp', 'tensor'), parts along dimension 0
- draft_feat: bfloat16 [64, 8, 8192], P('dp', None, 'tensor'), parts along dimension 0
There are 16 independent parts, one for each index of `dp`. A program takes and returns all parts, laid end to end along the dimension named above; an argument that names none is the same for every part. Nothing has to cross between parts.
Inputs may be any that keep to these rules, and one draw needn't show every extreme that they name: `q_rows`: float queries of order one; in the hidden draw some rows are scaled up strongly. `parents`: nodes 1 to 7 form a chain (parent of node i is i - 1); every later node has a parent below 7; entry 0 is 0. `cache_len`: in every group some request has all 8192 positions valid. `accepted_node`: in every group some request accepts node 7, whose path holds 8 nodes.
All inputs are finite; a program needn't handle non-finite values.
Results may differ from a plain program's by a relative error of at most 0.0075.
Values may be sent and summed in bfloat16 or wider, within the bound.
No kernel may reach another device: no remote copies, remote signals or barrier semaphores. Data moves between devices by JAX's collectives and lax.ppermute only.
A program may use at most 64 MiB of HBM per device.

v0:
```python
import jax
import jax.numpy as jnp
from jax import lax
from jax.sharding import PartitionSpec as P

D = 8192
HD = 128
HEADS_DEV = 1
KVH = 4
TREE = 16
MAXACC = 8


floor_score = -1e30
epsilon = 1e-05


def copy_for_each(x, axis):
    copies = jnp.broadcast_to(x, (lax.axis_size(axis), *x.shape))
    return lax.all_to_all(copies, axis, split_axis=0, concat_axis=0, tiled=True)


def in_order(tiles, dim):
    shape = list(tiles.shape[1:])
    shape[dim] *= tiles.shape[0]
    return jnp.moveaxis(tiles, 0, dim).reshape(shape)


def gather_directly(x, axis, dim):
    tiles = copy_for_each(x, axis)
    return in_order(tiles, dim)


def cut_along(x, dim, size):
    shape = x.shape
    tiles = x.reshape(*shape[:dim], size, shape[dim] // size, *shape[dim + 1 :])
    return jnp.moveaxis(tiles, dim, 0)


def sum_at_owner(x, axis, dim):
    tiles = cut_along(x, dim, lax.axis_size(axis))
    arrived = lax.all_to_all(tiles, axis, split_axis=0, concat_axis=0, tiled=True)
    return arrived.sum(axis=0)


def taken_together(x, axis):
    return copy_for_each(x, axis).sum(axis=0)


def ancestors(parents):
    nodes = jnp.arange(TREE, dtype=jnp.int32)
    link = (parents[:, :, None] == nodes[None, None, :]) & (nodes[None, :, None] > 0)
    reach = jnp.minimum(jnp.eye(TREE, dtype=jnp.float32)[None] + link.astype(jnp.float32), 1.0)
    for sweep in range((TREE - 1).bit_length()):
        reach = jnp.minimum(
            jnp.einsum("rab,rbc->rac", reach, reach, precision=lax.Precision.HIGHEST), 1.0
        )
    return reach


def path_select(reach, accepted_node):
    depth = jnp.sum(reach, axis=2) - 1.0
    onehot = (jnp.arange(TREE, dtype=jnp.int32)[None, :] == accepted_node[:, None]).astype(
        jnp.float32
    )
    onpath = jnp.einsum("rt,rtu->ru", onehot, reach, precision=lax.Precision.HIGHEST)
    levels = jnp.arange(MAXACC).astype(jnp.float32)
    return onpath[:, None, :] * (depth[:, None, :] == levels[None, :, None]).astype(jnp.float32)


def combine(earlier, later):
    top = jnp.maximum(earlier[0], later[0])
    first = jnp.exp(earlier[0] - top)
    second = jnp.exp(later[0] - top)
    return (
        top,
        earlier[1] * first + later[1] * second,
        earlier[2] * first[..., None] + later[2] * second[..., None],
    )


def on_device(
    q_rows,
    k_cache,
    v_cache,
    k_tree,
    v_tree,
    residual,
    wo_rows,
    gain,
    parents,
    cache_len,
    accepted_node,
):
    rank_here = lax.axis_index("tensor")
    req_count, cache_dev, kv_width = k_cache.shape
    num_rows = q_rows.shape[0]
    tree_size = num_rows // req_count
    col_share = residual.shape[1]
    score_scale = HD ** (-0.5)
    q_all = gather_directly(q_rows, "tensor", 1)
    head_count = q_all.shape[1] // HD
    group_size = head_count // KVH
    q_view = q_all.reshape(req_count, tree_size, KVH, group_size, HD)
    cache_keys = k_cache.reshape(req_count, cache_dev, KVH, HD)
    cache_values = v_cache.reshape(req_count, cache_dev, KVH, HD)
    scores = (
        jnp.einsum("rtkgd,rckd->kgrtc", q_view, cache_keys, preferred_element_type=jnp.float32)
        * score_scale
    )
    positions = rank_here * cache_dev + jnp.arange(cache_dev, dtype=jnp.int32)
    valid = (positions[None, :] < cache_len[:, None])[None, None, :, None, :]
    local_max = jnp.max(jnp.where(valid, scores, floor_score), axis=4)
    weights = jnp.where(valid, jnp.exp(scores - local_max[..., None]), 0.0)
    local_sum = jnp.sum(weights, axis=4)
    local_acc = jnp.einsum(
        "kgrtc,rckd->kgrtd",
        weights.astype(jnp.bfloat16),
        cache_values,
        preferred_element_type=jnp.float32,
    )
    part_max = local_max.reshape(head_count, num_rows)
    part_sum = local_sum.reshape(head_count, num_rows)
    part_acc = local_acc.reshape(head_count, num_rows, HD)
    recv_max, recv_sum, recv_acc = (
        lax.all_to_all(part_max, "tensor", split_axis=0, concat_axis=0, tiled=True),
        lax.all_to_all(part_sum, "tensor", split_axis=0, concat_axis=0, tiled=True),
        lax.all_to_all(part_acc, "tensor", split_axis=0, concat_axis=0, tiled=True),
    )
    recv_max = recv_max.reshape(-1, HEADS_DEV, num_rows)
    recv_sum = recv_sum.reshape(-1, HEADS_DEV, num_rows)
    recv_acc = recv_acc.reshape(-1, HEADS_DEV, num_rows, HD)
    own_max = jnp.max(recv_max, axis=0)
    factor = jnp.exp(recv_max - own_max[None])
    own_sum = jnp.sum(recv_sum * factor, axis=0)
    own_acc = jnp.sum(recv_acc * factor[..., None], axis=0)
    reach = ancestors(parents)
    own_q = q_rows.reshape(req_count, tree_size, HEADS_DEV, HD)
    kv_index = rank_here * HEADS_DEV // group_size
    tree_keys = lax.dynamic_slice_in_dim(
        k_tree.reshape(req_count, tree_size, KVH, HD), kv_index, 1, 2
    )[:, :, 0]
    tree_values = lax.dynamic_slice_in_dim(
        v_tree.reshape(req_count, tree_size, KVH, HD), kv_index, 1, 2
    )[:, :, 0]
    tree_scores = (
        jnp.einsum("rtjd,rud->jrtu", own_q, tree_keys, preferred_element_type=jnp.float32)
        * score_scale
    )
    tree_valid = (reach > 0.5)[None]
    tree_max = jnp.max(jnp.where(tree_valid, tree_scores, floor_score), axis=3)
    tree_weights = jnp.where(tree_valid, jnp.exp(tree_scores - tree_max[..., None]), 0.0)
    tree_sum = jnp.sum(tree_weights, axis=3).reshape(HEADS_DEV, num_rows)
    tree_acc = jnp.einsum(
        "jrtu,rud->jrtd",
        tree_weights.astype(jnp.bfloat16),
        tree_values,
        preferred_element_type=jnp.float32,
    )
    joined = combine(
        (own_max, own_sum, own_acc),
        (
            tree_max.reshape(HEADS_DEV, num_rows),
            tree_sum,
            tree_acc.reshape(HEADS_DEV, num_rows, HD),
        ),
    )
    attention = (joined[2] / joined[1][..., None]).astype(jnp.bfloat16)
    attention = jnp.transpose(attention, (1, 0, 2)).reshape(num_rows, HEADS_DEV * HD)
    term = jnp.dot(attention, wo_rows, preferred_element_type=jnp.float32)
    own_cols = lax.dynamic_slice_in_dim(
        term, rank_here * col_share, col_share, 1
    ) + residual.astype(jnp.float32)
    term = lax.dynamic_update_slice_in_dim(term, own_cols, rank_here * col_share, 1)
    hidden = sum_at_owner(term, "tensor", 1)
    square_total = taken_together(jnp.sum(hidden * hidden, axis=1), "tensor")
    mean_square = square_total / D
    layer_out = hidden.astype(jnp.bfloat16)
    features = (
        hidden * lax.rsqrt(mean_square + epsilon)[:, None] * gain.astype(jnp.float32)[None, :]
    ).astype(jnp.bfloat16)
    select = path_select(reach, accepted_node).astype(jnp.bfloat16)
    draft_feat = jnp.einsum(
        "rat,rtc->rac",
        select,
        features.reshape(req_count, tree_size, col_share),
        preferred_element_type=jnp.float32,
    )
    return (layer_out, draft_feat.astype(jnp.bfloat16))


def solution(mesh):
    return jax.shard_map(
        on_device,
        mesh=mesh,
        in_specs=(
            P("dp", "tensor"),
            P("dp", "tensor", None),
            P("dp", "tensor", None),
            P("dp", None, None),
            P("dp", None, None),
            P("dp", "tensor"),
            P("tensor", None),
            P("tensor"),
            P("dp", None),
            P("dp"),
            P("dp"),
        ),
        out_specs=(P("dp", "tensor"), P("dp", None, "tensor")),
        check_vma=False,
    )
```

profile of v0, /device:TPU:320, one launch (start us, length us, event | category | flops | bytes accessed | tf_op | source)
XLA Modules:
  0.0 167.9 jit_solution(11343845461328080360)
XLA Ops:
  0.6 0.0 copy-start
  0.6 0.0 copy-start.2
  0.7 0.0 copy-start.7
  0.7 1.8 %broadcast_in_dim.32 = bf16[32,64,128]{2,1,0:T(8,128)(2,1)} broadcast(bf16[64,128]{1,0:T(8,128)(2,1)} %param.11), dimensions={1,2} | broadcast | bytes 540672 | tf_op jit(solution)/shard_map/broadcast_in_dim | solution.py:19
  2.5 10.1 %all-to-all-start = ((bf16[32,64,128]{2,1,0:T(8,128)(2,1)}), bf16[32,64,128]{2,1,0:T(8,128)(2,1)}, u32[]{:S(2)}, u32[]{:S(2)}) async-start(bf16[32,64,128]{2,1,0:T(8,128)(2,1)} %broadcast_in_dim.32), calls=%async_computation | async-start | bytes 1048576 | tf_op jit(solution)/shard_map/all_to_all | solution.py:20
  12.6 0.9 reshape.270
  13.4 0.0 copy-done.2
  13.4 1.1 reshape.267
  14.6 0.0 copy-done.7
  14.6 0.1 broadcast_compare_fusion.1
  14.7 14.5 %all-to-all-done = bf16[32,64,128]{2,1,0:T(8,128)(2,1)} async-done(((bf16[32,64,128]{2,1,0:T(8,128)(2,1)}), bf16[32,64,128]{2,1,0:T(8,128)(2,1)}, u32[]{:S(2)}, u32[]{:S(2)}) %all-to-all-start) | async-done | bytes 524320 | tf_op jit(solution)/shard_map/all_to_all | solution.py:20
  29.2 1.9 %fusion = (f32[4,8,4,16]{3,1,2,0:T(8,128)S(1)}, f32[4,4,256,16,8]{2,3,4,1,0:T(8,128)S(1)}) fusion(pred[4,256]{1,0:T(4,128)(4,1)S(1)} %broadcast_compare_fusion.1, bf16[4,16,4,8,128]{4,1,0,3,2:T(8,128)(2,1)} %bitcast.3, bf16[4,256,4,128,1]{3,2,1,0,4:T(4,128)(2,1)} %bitcast.88), kind=kOutput, calls=%fused_computation.3 | convolution fusion | flops 135788544 | bytes 3679232 | tf_op jit(solution)/shard_map/rtkgd,rckd->kgrtc/dot_general | solution.py:108
  31.2 0.0 copy-start.1
  31.2 0.0 copy-start.3
  31.2 1.3 copy-done.1
  32.5 0.8 fusion.3
  33.4 0.7 all_to_all.29
  34.1 5.8 %all-to-all-start.3 = ((f32[32,1,64]{2,1,0:T(1,128)}), f32[32,1,64]{2,1,0:T(1,128)S(1)}, u32[]{:S(2)}, u32[]{:S(2)}) async-start(f32[32,1,64]{2,1,0:T(1,128)} %bitcast.21), calls=%async_computation.3 | async-start | bytes 32768 | tf_op jit(solution)/shard_map/all_to_all | solution.py:127
  39.9 0.0 copy-done.3
  39.9 1.1 reshape.268
  41.0 0.7 all_to_all.27
  41.7 7.9 %all-to-all-done.3 = f32[32,1,64]{2,1,0:T(1,128)S(1)} async-done(((f32[32,1,64]{2,1,0:T(1,128)}), f32[32,1,64]{2,1,0:T(1,128)S(1)}, u32[]{:S(2)}, u32[]{:S(2)}) %all-to-all-start.3) | async-done | bytes 8224 | tf_op jit(solution)/shard_map/all_to_all | solution.py:127
  49.6 3.8 %all-to-all-start.2 = ((f32[32,1,64]{2,1,0:T(1,128)}), f32[32,1,64]{2,1,0:T(1,128)S(1)}, u32[]{:S(2)}, u32[]{:S(2)}) async-start(f32[32,1,64]{2,1,0:T(1,128)} %bitcast.8), calls=%async_computation.2 | async-start | bytes 32768 | tf_op jit(solution)/shard_map/all_to_all | solution.py:126
  53.4 2.5 %convolution_bitcast_fusion = f32[4,8,4,16,128]{4,3,1,2,0:T(8,128)S(1)} fusion(f32[4,4,256,16,8]{2,3,4,1,0:T(8,128)} %copy-done.1, bf16[4,256,4,128,1]{3,2,1,0,4:T(4,128)(2,1)} %bitcast.89, f32[4,8,4,16]{3,1,2,0:T(8,128)S(1)} %get-tuple-element.12, pred[4,256]{1,0:T(4,128)(4,1)S(1)} %broadcast_compare_fusion.1), kind=kOutput, calls=%fused_computation.8 | convolution fusion | flops 136314880 | bytes 4203520 | tf_op jit(solution)/shard_map/kgrtc,rckd->kgrtd/dot_general | solution.py:116
  55.9 0.0 copy-start.8
  56.0 0.0 copy-start.6
  56.0 0.0 copy-start.4
  56.0 1.1 copy.75
  57.1 6.1 %all-to-all-done.2 = f32[32,1,64]{2,1,0:T(1,128)S(1)} async-done(((f32[32,1,64]{2,1,0:T(1,128)}), f32[32,1,64]{2,1,0:T(1,128)S(1)}, u32[]{:S(2)}, u32[]{:S(2)}) %all-to-all-start.2) | async-done | bytes 8224 | tf_op jit(solution)/shard_map/all_to_all | solution.py:126
  63.2 3.9 %all-to-all-start.1 = ((f32[32,64,128]{2,1,0:T(8,128)}), f32[32,64,128]{2,1,0:T(8,128)S(1)}, u32[]{:S(2)}, u32[]{:S(2)}) async-start(f32[32,64,128]{2,1,0:T(8,128)} %bitcast.7), calls=%async_computation.1 | async-start | bytes 2097152 | tf_op jit(solution)/shard_map/all_to_all | solution.py:128
  67.1 0.0 copy-done.8
  67.1 0.2 convolution_minimum_fusion.3
  67.4 0.2 convolution_minimum_fusion.2
  67.5 0.2 convolution_minimum_fusion.1
  67.7 0.2 fusion.53
  68.0 0.0 copy-done.6
  68.0 0.2 select_reduce_fusion
  68.2 0.1 reshape.272
  68.3 0.2 fusion.25
  68.4 0.1 reshape.276
  68.5 0.0 copy-done.4
  68.6 0.2 fusion.28
  68.8 0.1 reduce_max.28
  68.9 0.1 multiply_reduce_fusion.2
  68.9 24.2 %all-to-all-done.1 = f32[32,64,128]{2,1,0:T(8,128)S(1)} async-done(((f32[32,64,128]{2,1,0:T(8,128)}), f32[32,64,128]{2,1,0:T(8,128)S(1)}, u32[]{:S(2)}, u32[]{:S(2)}) %all-to-all-start.1) | async-done | bytes 1048608 | tf_op jit(solution)/shard_map/all_to_all | solution.py:128
  93.2 0.3 multiply_reduce_fusion
  93.5 0.1 fusion.17
  93.6 0.0 copy-done
  93.6 0.0 copy-start.5
  93.6 0.4 fusion.54
  94.1 0.3 copy-done.5
  94.4 1.5 copy.121
  95.9 5.3 %all-to-all-start.4 = ((f32[32,64,256]{2,1,0:T(8,128)}), f32[32,64,256]{2,1,0:T(8,128)}, u32[]{:S(2)}, u32[]{:S(2)}) async-start(f32[32,64,256]{2,1,0:T(8,128)} %bitcast.87), calls=%async_computation.4 | async-start | bytes 4194304 | tf_op jit(solution)/shard_map/all_to_all | solution.py:42
  101.3 0.0 copy-start.10
  101.3 0.1 fusion.43
  101.3 0.1 fusion.41
  101.5 47.3 %all-to-all-done.4 = f32[32,64,256]{2,1,0:T(8,128)} async-done(((f32[32,64,256]{2,1,0:T(8,128)}), f32[32,64,256]{2,1,0:T(8,128)}, u32[]{:S(2)}, u32[]{:S(2)}) %all-to-all-start.4) | async-done | bytes 2097184 | tf_op jit(solution)/shard_map/all_to_all | solution.py:42
  148.7 1.7 %reduce_sum.78 = f32[64,256]{1,0:T(8,128)S(1)} reduce(f32[32,64,256]{2,1,0:T(8,128)} %all-to-all-done.4, f32[]{:T(128)} %constant.15.clone.1), dimensions={0}, to_apply=%region_7.8 | reduce | flops 507904 | bytes 2162692 | tf_op jit(solution)/shard_map/reduce_sum | solution.py:43
  150.5 0.7 multiply_reduce_fusion.1
  151.2 0.6 broadcast_in_dim.62
  151.8 5.4 %all-to-all-start.5 = ((f32[32,1,64]{2,1,0:T(1,128)}), f32[32,1,64]{2,1,0:T(1,128)S(1)}, u32[]{:S(2)}, u32[]{:S(2)}) async-start(f32[32,1,64]{2,1,0:T(1,128)} %broadcast_in_dim.62), calls=%async_computation.5 | async-start | bytes 32768 | tf_op jit(solution)/shard_map/all_to_all | solution.py:20
  157.3 9.7 %all-to-all-done.5 = f32[32,1,64]{2,1,0:T(1,128)S(1)} async-done(((f32[32,1,64]{2,1,0:T(1,128)}), f32[32,1,64]{2,1,0:T(1,128)S(1)}, u32[]{:S(2)}, u32[]{:S(2)}) %all-to-all-start.5) | async-done | bytes 8224 | tf_op jit(solution)/shard_map/all_to_all | solution.py:20
  167.0 0.1 rsqrt.11
  167.1 0.8 convolution_convert_fusion
  (18 shorter events, 0.2 us)
Async XLA Ops:
  0.6 93.0 %copy-start = (bf16[128,8192]{1,0:T(8,128)(2,1)S(1)}, bf16[128,8192]{1,0:T(8,128)(2,1)}, u32[]{:S(2)}) copy-start(bf16[128,8192]{1,0:T(8,128)(2,1)} %param.17) | copy-start | bytes 6291460
  0.6 12.8 %copy-start.2 = (bf16[4,256,512]{2,1,0:T(8,128)(2,1)S(1)}, bf16[4,256,512]{2,1,0:T(8,128)(2,1)}, u32[]{:S(2)}) copy-start(bf16[4,256,512]{2,1,0:T(8,128)(2,1)} %param.12) | copy-start | bytes 3145732
  0.7 14.0 %copy-start.7 = (s32[4]{0:T(128)S(1)}, s32[4]{0:T(128)}, u32[]{:S(2)}) copy-start(s32[4]{0:T(128)} %param.20) | copy-start | bytes 52
  2.5 26.8 %all-to-all-start = ((bf16[32,64,128]{2,1,0:T(8,128)(2,1)}), bf16[32,64,128]{2,1,0:T(8,128)(2,1)}, u32[]{:S(2)}, u32[]{:S(2)}) async-start(bf16[32,64,128]{2,1,0:T(8,128)(2,1)} %broadcast_in_dim.32), calls=%async_computation | async-start | bytes 1048576 | tf_op jit(solution)/shard_map/all_to_all | solution.py:20
  31.2 1.4 copy-start.1
  31.2 8.7 %copy-start.3 = (bf16[4,256,512]{2,1,0:T(8,128)(2,1)S(1)}, bf16[4,256,512]{2,1,0:T(8,128)(2,1)}, u32[]{:S(2)}) copy-start(bf16[4,256,512]{2,1,0:T(8,128)(2,1)} %param.13) | copy-start | bytes 3145732
  34.1 15.5 %all-to-all-start.3 = ((f32[32,1,64]{2,1,0:T(1,128)}), f32[32,1,64]{2,1,0:T(1,128)S(1)}, u32[]{:S(2)}, u32[]{:S(2)}) async-start(f32[32,1,64]{2,1,0:T(1,128)} %bitcast.21), calls=%async_computation.3 | async-start | bytes 32768 | tf_op jit(solution)/shard_map/all_to_all | solution.py:127
  49.6 13.6 %all-to-all-start.2 = ((f32[32,1,64]{2,1,0:T(1,128)}), f32[32,1,64]{2,1,0:T(1,128)S(1)}, u32[]{:S(2)}, u32[]{:S(2)}) async-start(f32[32,1,64]{2,1,0:T(1,128)} %bitcast.8), calls=%async_computation.2 | async-start | bytes 32768 | tf_op jit(solution)/shard_map/all_to_all | solution.py:126
  55.9 11.2 %copy-start.8 = (s32[4,16]{1,0:T(4,128)S(1)}, s32[4,16]{1,0:T(4,128)}, u32[]{:S(2)}) copy-start(s32[4,16]{1,0:T(4,128)} %param.19) | copy-start | bytes 772
  56.0 12.0 %copy-start.6 = (bf16[64,128]{1,0:T(8,128)(2,1)S(1)}, bf16[64,128]{1,0:T(8,128)(2,1)}, u32[]{:S(2)}) copy-start(bf16[64,128]{1,0:T(8,128)(2,1)} %param.11) | copy-start | bytes 49156
  56.0 12.6 %copy-start.4 = (bf16[4,16,512]{2,1,0:T(8,128)(2,1)S(1)}, bf16[4,16,512]{2,1,0:T(8,128)(2,1)}, u32[]{:S(2)}) copy-start(bf16[4,16,512]{2,1,0:T(8,128)(2,1)} %param.15) | copy-start | bytes 196612
  63.2 30.0 %all-to-all-start.1 = ((f32[32,64,128]{2,1,0:T(8,128)}), f32[32,64,128]{2,1,0:T(8,128)S(1)}, u32[]{:S(2)}, u32[]{:S(2)}) async-start(f32[32,64,128]{2,1,0:T(8,128)} %bitcast.7), calls=%async_computation.1 | async-start | bytes 2097152 | tf_op jit(solution)/shard_map/all_to_all | solution.py:128
  93.6 0.8 copy-start.5
  95.9 5.3 %copy-start.9 = (s32[4]{0:T(128)S(1)}, s32[4]{0:T(128)}, u32[]{:S(2)}) copy-start(s32[4]{0:T(128)} %param.21) | copy-start | bytes 52
  95.9 52.8 %all-to-all-start.4 = ((f32[32,64,256]{2,1,0:T(8,128)}), f32[32,64,256]{2,1,0:T(8,128)}, u32[]{:S(2)}, u32[]{:S(2)}) async-start(f32[32,64,256]{2,1,0:T(8,128)} %bitcast.87), calls=%async_computation.4 | async-start | bytes 4194304 | tf_op jit(solution)/shard_map/all_to_all | solution.py:42
  101.3 56.0 %copy-start.10 = (bf16[256]{0:T(256)(128)(2,1)S(1)}, bf16[256]{0:T(256)(128)(2,1)}, u32[]{:S(2)}) copy-start(bf16[256]{0:T(256)(128)(2,1)} %param.18) | copy-start | bytes 1540
  151.8 15.1 %all-to-all-start.5 = ((f32[32,1,64]{2,1,0:T(1,128)}), f32[32,1,64]{2,1,0:T(1,128)S(1)}, u32[]{:S(2)}, u32[]{:S(2)}) async-start(f32[32,1,64]{2,1,0:T(1,128)} %broadcast_in_dim.62), calls=%async_computation.5 | async-start | bytes 32768 | tf_op jit(solution)/shard_map/all_to_all | solution.py:20
where the time goes:
time: 169 us; the launch traced here: 168 us
  waiting for transfers between devices  110 us (65%)
  starting transfers between devices  34.3 us (20%)
  local copies, waits for them, and re-layouts  11.7 us (7%)
  matrix products  7.03 us (4%)
  other arithmetic  4.2 us (2%)
    all_to_all x1, waiting for transfers between devices, sum_at_owner(): lax.all_to_all(tiles, axis, split_axis=0, concat_axis=0, tiled=True)  47.3 us
    all_to_all x1, waiting for transfers between devices, on_device(): lax.all_to_all(part_acc, 'tensor', split_axis=0, concat_axis=0, tiled=True)  24.2 us
    all_to_all x2, waiting for transfers between devices, copy_for_each(): return lax.all_to_all(copies, axis, split_axis=0, concat_axis=0, tiled=True)  24.2 us
    all_to_all x2, starting transfers between devices, copy_for_each(): return lax.all_to_all(copies, axis, split_axis=0, concat_axis=0, tiled=True)  15.5 us
    all_to_all x1, waiting for transfers between devices, on_device(): lax.all_to_all(part_sum, 'tensor', split_axis=0, concat_axis=0, tiled=True)  7.87 us
    all_to_all x1, waiting for transfers between devices, on_device(): lax.all_to_all(part_max, 'tensor', split_axis=0, concat_axis=0, tiled=True)  6.07 us
    all_to_all x1, starting transfers between devices, on_device(): lax.all_to_all(part_sum, 'tensor', split_axis=0, concat_axis=0, tiled=True)  5.77 us
    all_to_all x1, starting transfers between devices, sum_at_owner(): lax.all_to_all(tiles, axis, split_axis=0, concat_axis=0, tiled=True)  5.31 us
  transfers between devices with their start and end apart: 6, of which 6 were waited for; matrix products, arithmetic and copies ran while one was open for 5% of the time, Pallas kernels for 0%

commit v1 on v0

v1 whole, which is shorter than its diff:
```python
import jax
import jax.numpy as jnp
from jax import lax
from jax.experimental import pallas as pl
from jax.experimental.pallas import tpu as pltpu
from jax.sharding import PartitionSpec as P

D = 8192
HD = 128
KVH = 4
TREE = 16
REQ = 4
ROWS = REQ * TREE
MAXACC = 8
HEADS = 32
GROUP = HEADS // KVH
STAT = 8
MSG = ROWS + STAT

floor_score = -1e30
epsilon = 1e-05
score_scale = HD ** (-0.5)
f32 = jnp.float32
bf16 = jnp.bfloat16
VM = pl.BlockSpec(memory_space=pltpu.VMEM)
SM = pl.BlockSpec(memory_space=pltpu.SMEM)


def iota(shape, dim):
    return lax.broadcasted_iota(jnp.int32, shape, dim)


def three_parts(x):
    hi = x.astype(bf16).astype(f32)
    mid = (x - hi).astype(bf16).astype(f32)
    return hi, mid, x - hi - mid


def to_all(x):
    return lax.all_to_all(x, "tensor", split_axis=0, concat_axis=0, tiled=True)


def tree_kernel(rank, parents, q, kt, vt, acc_node, o_ref, lse_ref, sel_ref):
    row = iota((ROWS, ROWS), 0)
    col = iota((ROWS, ROWS), 1)
    same = (row // TREE) == (col // TREE)
    up = jnp.zeros((ROWS, ROWS), jnp.int32)
    for r in range(REQ):
        for i in range(1, TREE):
            up = jnp.where(row == r * TREE + i, parents[r, i] + r * TREE, up)
    link = jnp.where((up == col) & (row % TREE > 0), 1.0, 0.0)
    reach = jnp.where(row == col, 1.0, link)
    for sweep in range((TREE - 1).bit_length()):
        half = reach.astype(bf16)
        reach = jnp.minimum(jnp.dot(half, half, preferred_element_type=f32), 1.0)
    lane = pl.ds(pl.multiple_of((rank[0] // GROUP) * HD, HD), HD)
    keys = jnp.concatenate([kt[r, :, lane] for r in range(REQ)], axis=0)
    values = jnp.concatenate([vt[r, :, lane] for r in range(REQ)], axis=0)
    nt = (((1,), (1,)), ((), ()))
    scores = lax.dot_general(q[...], keys, nt, preferred_element_type=f32) * score_scale
    valid = (reach > 0.5) & same
    scores = jnp.where(valid, scores, floor_score)
    top = jnp.max(scores, axis=1, keepdims=True)
    e = jnp.where(valid, jnp.exp(scores - top), 0.0)
    total = jnp.sum(e, axis=1, keepdims=True)
    o_ref[...] = jnp.dot(e.astype(bf16), values, preferred_element_type=f32) / total
    lse = jnp.broadcast_to(top + jnp.log(total), (ROWS, HD))
    lse_ref[...] = lse.T[:8, :]
    depth = lax.dot_general(
        jnp.ones((8, ROWS), bf16), reach.astype(bf16), nt, preferred_element_type=f32
    )[:1, :] - 1.0
    out = iota((REQ * MAXACC, ROWS), 0)
    lanes = iota((REQ * MAXACC, ROWS), 1)
    chosen = jnp.zeros((REQ * MAXACC, ROWS), jnp.int32)
    for r in range(REQ):
        chosen = jnp.where(out // MAXACC == r, acc_node[r] + r * TREE, chosen)
    onehot = jnp.where(lanes == chosen, 1.0, 0.0).astype(bf16)
    onpath = jnp.dot(onehot, reach.astype(bf16), preferred_element_type=f32)
    level = (out % MAXACC).astype(f32)
    sel_ref[...] = jnp.where(depth == level, onpath, 0.0).astype(bf16)


def attend_kernel(rank, cache_len, q, k, v, out):
    span = k.shape[1]
    nt = (((1,), (1,)), ((), ()))
    tn = (((0,), (0,)), ((), ()))
    start = rank[0] * span
    pos = iota((span, HD), 0) + start
    sub = iota((GROUP, HD), 0)
    lane = iota((GROUP, HD), 1)
    for g in range(KVH):
        cols = slice(g * HD, (g + 1) * HD)
        packed = jnp.zeros((GROUP, HD), f32)
        for r in range(REQ):
            rows = slice(r * TREE, (r + 1) * TREE)
            qh = q[g * GROUP : (g + 1) * GROUP, rows, :].reshape(GROUP * TREE, HD)
            s = lax.dot_general(k[r, :, cols], qh, nt, preferred_element_type=f32) * score_scale
            valid = pos < cache_len[r]
            s = jnp.where(valid, s, floor_score)
            top = jnp.max(s, axis=0, keepdims=True)
            e = jnp.where(valid, jnp.exp(s - top), 0.0)
            total = jnp.sum(e, axis=0, keepdims=True)
            some = total > 0.0
            inv = jnp.where(some, 1.0 / jnp.where(some, total, 1.0), 0.0)
            lse = jnp.where(some, top + jnp.log(jnp.where(some, total, 1.0)), floor_score)
            p = (e * inv).astype(bf16)
            o = lax.dot_general(p, v[r, :, cols], tn, preferred_element_type=f32)
            out[g * GROUP : (g + 1) * GROUP, rows, :] = o.astype(bf16).reshape(GROUP, TREE, HD)
            turned = pltpu.roll(
                jnp.broadcast_to(pltpu.roll(lse, (r + 1) * TREE, 1), (GROUP, HD)),
                0,
                1,
                stride=TREE,
                stride_axis=0,
            )
            packed = jnp.where(lane // TREE == r, turned, packed)
        hi, mid, lo = three_parts(packed)
        first = jnp.where(lane < ROWS, hi, pltpu.roll(mid, ROWS, 1))
        for j in range(GROUP):
            i = GROUP - 1 - j
            stat = jnp.where(sub == 0, first[i : i + 1, :], jnp.where(sub == 1, lo[i : i + 1, :], 0.0))
            out[g * GROUP + j, ROWS:MSG, :] = stat.astype(bf16)


def project_kernel(got, o_tree, lse_tree, wo, out):
    srcs = got.shape[0]
    stats = got[:, ROWS:MSG, :].astype(f32)
    first = stats[:, 0, :]
    lse = first + pltpu.roll(first, ROWS, 1) + stats[:, 1, :]
    tree = lse_tree[0:1, :]
    tree = jnp.concatenate([tree, jnp.zeros((1, HD - ROWS), f32)], axis=1)
    top = jnp.maximum(jnp.max(lse, axis=0, keepdims=True), tree)
    w = jnp.exp(lse - top)
    wt = jnp.exp(tree - top)
    inv = 1.0 / (jnp.sum(w, axis=0, keepdims=True) + wt)
    every = jnp.concatenate(
        [w * inv, jnp.broadcast_to(wt * inv, (8, HD)), jnp.zeros((HD - srcs - 8, HD), f32)], axis=0
    ).T[:ROWS, :]
    att = o_tree[...] * every[:, srcs : srcs + 1]
    for c in range(srcs):
        att = att + got[c, :ROWS, :].astype(f32) * every[:, c : c + 1]
    att = att.astype(bf16)
    width = out.shape[2]
    for d in range(out.shape[0]):
        part = jnp.dot(att, wo[:, d * width : (d + 1) * width], preferred_element_type=f32)
        out[d] = part.astype(bf16)


def hidden_kernel(got, residual, h_ref, layer_ref, sq_ref):
    h = residual[...].astype(f32)
    for c in range(got.shape[0]):
        h = h + got[c].astype(f32)
    h_ref[...] = h
    layer_ref[...] = h.astype(bf16)
    sq = lax.dot_general(
        jnp.ones((8, h.shape[1]), f32),
        h * h,
        (((1,), (1,)), ((), ())),
        preferred_element_type=f32,
        precision=lax.Precision.HIGHEST,
    )
    sq_ref[...] = jnp.broadcast_to(sq[0:1, :][None], sq_ref.shape)


def draft_kernel(got, h, gain, sel, out):
    sq = got[...].reshape(got.shape[0], ROWS)
    total = lax.dot_general(
        sq,
        jnp.ones((got.shape[0], h.shape[1]), f32),
        (((0,), (0,)), ((), ())),
        preferred_element_type=f32,
        precision=lax.Precision.HIGHEST,
    )
    scale = lax.rsqrt(total / D + epsilon)
    feat = (h[...] * scale * gain[...].astype(f32)).astype(bf16)
    out[...] = jnp.dot(sel[...], feat, preferred_element_type=f32).astype(bf16)


def shape(dims, kind):
    return jax.ShapeDtypeStruct(dims, kind)


def on_device(
    q_rows,
    k_cache,
    v_cache,
    k_tree,
    v_tree,
    residual,
    wo_rows,
    gain,
    parents,
    cache_len,
    accepted_node,
):
    count = lax.axis_size("tensor")
    rank = lax.axis_index("tensor").astype(jnp.int32).reshape(1)
    width = residual.shape[1]
    q_all = to_all(jnp.broadcast_to(q_rows, (count, ROWS, HD)))
    o_tree, lse_tree, sel = pl.pallas_call(
        tree_kernel,
        name="tree",
        out_shape=(shape((ROWS, HD), f32), shape((8, ROWS), f32), shape((REQ * MAXACC, ROWS), bf16)),
        in_specs=[SM, SM, VM, VM, VM, SM],
        out_specs=(VM, VM, VM),
        cost_estimate=pl.CostEstimate(flops=10**8, bytes_accessed=300000, transcendentals=10000),
    )(rank, parents, q_rows, k_tree, v_tree, accepted_node)
    sent = pl.pallas_call(
        attend_kernel,
        name="attend",
        out_shape=shape((HEADS, MSG, HD), bf16),
        in_specs=[SM, SM, VM, VM, VM],
        out_specs=VM,
    )(rank, cache_len, q_all, k_cache, v_cache)
    got = to_all(sent)
    terms = pl.pallas_call(
        project_kernel,
        name="project",
        out_shape=shape((count, ROWS, width), bf16),
        in_specs=[VM, VM, VM, VM],
        out_specs=VM,
    )(got, o_tree, lse_tree, wo_rows)
    arrived = to_all(terms)
    h, layer_out, squares = pl.pallas_call(
        hidden_kernel,
        name="hidden",
        out_shape=(shape((ROWS, width), f32), shape((ROWS, width), bf16), shape((count, 1, ROWS), f32)),
        in_specs=[VM, VM],
        out_specs=(VM, VM, VM),
    )(arrived, residual)
    totals = to_all(squares)
    draft = pl.pallas_call(
        draft_kernel,
        name="draft",
        out_shape=shape((REQ * MAXACC, width), bf16),
        in_specs=[VM, VM, VM, VM],
        out_specs=VM,
    )(totals, h, gain.reshape(1, width), sel)
    return (layer_out, draft.reshape(REQ, MAXACC, width))


def solution(mesh):
    return jax.shard_map(
        on_device,
        mesh=mesh,
        in_specs=(
            P("dp", "tensor"),
            P("dp", "tensor", None),
            P("dp", "tensor", None),
            P("dp", None, None),
            P("dp", None, None),
            P("dp", "tensor"),
            P("tensor", None),
            P("tensor"),
            P("dp", None),
            P("dp"),
            P("dp"),
        ),
        out_specs=(P("dp", "tensor"), P("dp", None, "tensor")),
        check_vma=False,
    )
```

time: 169 us -> 116 us (0.69)
  the two profiles are of different devices: /device:TPU:320 before, /device:TPU:1 now
where the time goes in v1:
time: 116 us; the launch traced here: 114 us
  waiting for transfers between devices  35.3 us (30%)
  blocking collectives  33.2 us (29%)
  starting transfers between devices  25.6 us (22%)
  Pallas kernels  14.6 us (13%)
  local copies, waits for them, and re-layouts  4.46 us (4%)
    all_to_all x3, waiting for transfers between devices, to_all(): return lax.all_to_all(x, 'tensor', split_axis=0, concat_axis=0, tiled=True)  35.3 us
    all_to_all x1, blocking collectives, to_all(): return lax.all_to_all(x, 'tensor', split_axis=0, concat_axis=0, tiled=True)  33.2 us
    all_to_all x3, starting transfers between devices, to_all(): return lax.all_to_all(x, 'tensor', split_axis=0, concat_axis=0, tiled=True)  25.6 us
    pallas_call x1, Pallas kernels, on_device(): pl.pallas_call(attend_kernel, name='attend', out_shape=shape((HEADS, MSG,...  4.48 us
    pallas_call x1, Pallas kernels, on_device(): pl.pallas_call(project_kernel, name='project', out_shape=shape((count, RO...  3.85 us
  transfers between devices with their start and end apart: 3, of which 3 were waited for; matrix products, arithmetic and copies ran while one was open for 1% of the time, Pallas kernels for 2%

profile of v1, /device:TPU:1, one launch (start us, length us, event | category | flops | bytes accessed | tf_op | source)
XLA Modules:
  0.0 113.9 jit_solution(9482696109734258318)
XLA Ops:
  0.6 1.6 %broadcast_in_dim.3 = bf16[32,64,128]{2,1,0:T(8,128)(2,1)} broadcast(bf16[64,128]{1,0:T(8,128)(2,1)} %q.1), dimensions={1,2} | broadcast | bytes 540672 | tf_op jit(solution)/shard_map/broadcast_in_dim | solution.py:199
  2.3 10.5 %all-to-all-start = ((bf16[32,64,128]{2,1,0:T(8,128)(2,1)}), bf16[32,64,128]{2,1,0:T(8,128)(2,1)S(1)}, u32[]{:S(2)}, u32[]{:S(2)}) async-start(bf16[32,64,128]{2,1,0:T(8,128)(2,1)} %broadcast_in_dim.3), calls=%async_computation | async-start | bytes 1048576 | tf_op jit(solution)/shard_map/all_to_all | solution.py:40
  12.8 14.5 %all-to-all-done.q = bf16[32,64,128]{2,1,0:T(8,128)(2,1)S(1)} async-done(((bf16[32,64,128]{2,1,0:T(8,128)(2,1)}), bf16[32,64,128]{2,1,0:T(8,128)(2,1)S(1)}, u32[]{:S(2)}, u32[]{:S(2)}) %all-to-all-start) | async-done | bytes 524320 | tf_op jit(solution)/shard_map/all_to_all | solution.py:40
  27.3 0.0 copy-start.1
  27.3 0.8 copy-done.1
  28.1 4.5 %attend.1 = bf16[32,72,128]{2,1,0:T(8,128)(2,1)} custom-call(s32[1]{0:T(128)} %bitcast.rank, s32[4]{0:T(128)} %cache_len.1, bf16[32,64,128]{2,1,0:T(8,128)(2,1)} %copy-done.1, bf16[4,256,512]{2,1,0:T(8,128)(2,1)} %k.1, bf16[4,256,512]{2,1,0:T(8,128)(2,1)} %v.1), custom_call_target="tpu_custom_call" | custom-call | tf_op jit(solution)/shard_map/attend/pallas_call | solution.py:208
  32.6 7.3 %all-to-all-start.1 = ((bf16[32,72,128]{2,1,0:T(8,128)(2,1)}), bf16[32,72,128]{2,1,0:T(8,128)(2,1)S(1)}, u32[]{:S(2)}, u32[]{:S(2)}) async-start(bf16[32,72,128]{2,1,0:T(8,128)(2,1)} %attend.1), calls=%async_computation.1 | async-start | bytes 1179648 | tf_op jit(solution)/shard_map/all_to_all | solution.py:40
  39.8 2.3 %tree.1 = (f32[64,128]{1,0:T(8,128)}, f32[8,64]{1,0:T(8,128)}, bf16[32,64]{1,0:T(8,128)(2,1)}) custom-call(s32[1]{0:T(128)} %bitcast.rank, s32[4,16]{1,0:T(4,128)} %parents.1, bf16[64,128]{1,0:T(8,128)(2,1)} %q.1, bf16[4,16,512]{2,1,0:T(8,128)(2,1)} %kt.1, bf16[4,16,512]{2,1,0:T(8,128)(2,1)} %vt.1, s32[4]{0:T(128)} %acc_node.1), custom_call_target="tpu_custom_call" | custom-call | flops 100000000 | bytes 300000 | tf_op jit(solution)/shard_map/tree/pallas_call | solution.py:200
  42.1 12.8 %all-to-all-done.1.got = bf16[32,72,128]{2,1,0:T(8,128)(2,1)S(1)} async-done(((bf16[32,72,128]{2,1,0:T(8,128)(2,1)}), bf16[32,72,128]{2,1,0:T(8,128)(2,1)S(1)}, u32[]{:S(2)}, u32[]{:S(2)}) %all-to-all-start.1) | async-done | bytes 589856 | tf_op jit(solution)/shard_map/all_to_all | solution.py:40
  54.9 0.0 copy-start
  54.9 0.9 copy-done
  55.7 3.9 %project.1 = bf16[32,64,256]{2,1,0:T(8,128)(2,1)} custom-call(bf16[32,72,128]{2,1,0:T(8,128)(2,1)} %copy-done, f32[64,128]{1,0:T(8,128)} %get-tuple-element.8.o_tree, f32[8,64]{1,0:T(8,128)} %get-tuple-element.9.lse_tree, bf16[128,8192]{1,0:T(8,128)(2,1)} %wo.1), custom_call_target="tpu_custom_call" | custom-call | tf_op jit(solution)/shard_map/project/pallas_call | solution.py:216
  59.6 0.0 copy-start.3
  59.6 33.2 %all_to_all.20.got = bf16[32,64,256]{2,1,0:T(8,128)(2,1)} all-to-all(bf16[32,64,256]{2,1,0:T(8,128)(2,1)} %project.1), channel_id=1, replica_groups=mesh['dp'=16,'tensor'=32] {'tensor'}, dimensions={0} | all-to-all | bytes 2097152 | tf_op jit(solution)/shard_map/all_to_all | solution.py:40
  92.8 2.2 %hidden.1 = (f32[64,256]{1,0:T(8,128)}, bf16[64,256]{1,0:T(8,128)(2,1)}, f32[32,1,64]{2,1,0:T(1,128)}) custom-call(bf16[32,64,256]{2,1,0:T(8,128)(2,1)} %all_to_all.20.got, bf16[64,256]{1,0:T(8,128)(2,1)} %residual.1), custom_call_target="tpu_custom_call" | custom-call | tf_op jit(solution)/shard_map/hidden/pallas_call | solution.py:224
  95.0 7.9 %all-to-all-start.3 = ((f32[32,1,64]{2,1,0:T(1,128)}), f32[32,1,64]{2,1,0:T(1,128)S(1)}, u32[]{:S(2)}, u32[]{:S(2)}) async-start(f32[32,1,64]{2,1,0:T(1,128)} %get-tuple-element.11), calls=%async_computation.3 | async-start | bytes 32768 | tf_op jit(solution)/shard_map/all_to_all | solution.py:40
  102.9 0.0 copy-done.3
  102.9 0.6 reshape.14.gain
  103.5 8.0 %all-to-all-done.3.got = f32[32,1,64]{2,1,0:T(1,128)S(1)} async-done(((f32[32,1,64]{2,1,0:T(1,128)}), f32[32,1,64]{2,1,0:T(1,128)S(1)}, u32[]{:S(2)}, u32[]{:S(2)}) %all-to-all-start.3) | async-done | bytes 8224 | tf_op jit(solution)/shard_map/all_to_all | solution.py:40
  111.5 0.0 copy-start.2
  111.5 0.6 copy-done.2
  112.1 1.8 %draft.1 = bf16[32,256]{1,0:T(8,128)(2,1)} custom-call(f32[32,1,64]{2,1,0:T(1,128)} %copy-done.2, f32[64,256]{1,0:T(8,128)} %get-tuple-element.12.h, bf16[1,256]{1,0:T(2,128)(2,1)} %reshape.14.gain, bf16[32,64]{1,0:T(8,128)(2,1)} %get-tuple-element.13.sel), custom_call_target="tpu_custom_call" | custom-call | tf_op jit(solution)/shard_map/draft/pallas_call | solution.py:232
Async XLA Ops:
  2.3 25.0 %all-to-all-start = ((bf16[32,64,128]{2,1,0:T(8,128)(2,1)}), bf16[32,64,128]{2,1,0:T(8,128)(2,1)S(1)}, u32[]{:S(2)}, u32[]{:S(2)}) async-start(bf16[32,64,128]{2,1,0:T(8,128)(2,1)} %broadcast_in_dim.3), calls=%async_computation | async-start | bytes 1048576 | tf_op jit(solution)/shard_map/all_to_all | solution.py:40
  27.3 0.8 copy-start.1
  32.6 22.3 %all-to-all-start.1 = ((bf16[32,72,128]{2,1,0:T(8,128)(2,1)}), bf16[32,72,128]{2,1,0:T(8,128)(2,1)S(1)}, u32[]{:S(2)}, u32[]{:S(2)}) async-start(bf16[32,72,128]{2,1,0:T(8,128)(2,1)} %attend.1), calls=%async_computation.1 | async-start | bytes 1179648 | tf_op jit(solution)/shard_map/all_to_all | solution.py:40
  54.9 0.9 copy-start
  59.6 43.3 %copy-start.3 = (bf16[256]{0:T(256)(128)(2,1)S(1)}, bf16[256]{0:T(256)(128)(2,1)}, u32[]{:S(2)}) copy-start(bf16[256]{0:T(256)(128)(2,1)} %param.18) | copy-start | bytes 1540
  95.0 16.5 %all-to-all-start.3 = ((f32[32,1,64]{2,1,0:T(1,128)}), f32[32,1,64]{2,1,0:T(1,128)S(1)}, u32[]{:S(2)}, u32[]{:S(2)}) async-start(f32[32,1,64]{2,1,0:T(1,128)} %get-tuple-element.11), calls=%async_computation.3 | async-start | bytes 32768 | tf_op jit(solution)/shard_map/all_to_all | solution.py:40
  111.5 0.6 copy-start.2

commit v2 on v1

--- a/solution.py
+++ b/solution.py
@@ -24,6 +24,7 @@
 bf16 = jnp.bfloat16
 VM = pl.BlockSpec(memory_space=pltpu.VMEM)
 SM = pl.BlockSpec(memory_space=pltpu.SMEM)
+STAGGER = 12000
 
 
 def iota(shape, dim):
@@ -40,7 +41,20 @@
     return lax.all_to_all(x, "tensor", split_axis=0, concat_axis=0, tiled=True)
 
 
-def tree_kernel(rank, parents, q, kt, vt, acc_node, o_ref, lse_ref, sel_ref):
+def spread_kernel(late, q, out):
+    @pl.when(late[0] > 0)
+    def _():
+        pl.delay(STAGGER)
+
+    for d in range(out.shape[0]):
+        out[d] = q[...]
+
+
+def tree_kernel(
+    rank, parents, acc_node, cache_len, q, kt, vt, k, v, o_ref, lse_ref, sel_ref, left_ref
+):
+    for r in range(REQ):
+        left_ref[r] = jnp.full((8, HD), cache_len[r] - rank[0] * k.shape[1], jnp.int32)
     row = iota((ROWS, ROWS), 0)
     col = iota((ROWS, ROWS), 1)
     same = (row // TREE) == (col // TREE)
@@ -80,22 +94,22 @@
     sel_ref[...] = jnp.where(depth == level, onpath, 0.0).astype(bf16)
 
 
-def attend_kernel(rank, cache_len, q, k, v, out):
+def attend_kernel(left, q, k, v, out):
     span = k.shape[1]
     nt = (((1,), (1,)), ((), ()))
     tn = (((0,), (0,)), ((), ()))
-    start = rank[0] * span
-    pos = iota((span, HD), 0) + start
+    pos = iota((span, HD), 0)
     sub = iota((GROUP, HD), 0)
     lane = iota((GROUP, HD), 1)
-    for g in range(KVH):
-        cols = slice(g * HD, (g + 1) * HD)
-        packed = jnp.zeros((GROUP, HD), f32)
-        for r in range(REQ):
-            rows = slice(r * TREE, (r + 1) * TREE)
-            qh = q[g * GROUP : (g + 1) * GROUP, rows, :].reshape(GROUP * TREE, HD)
+    packed = [jnp.zeros((GROUP, HD), f32)] * KVH
+    for r in range(REQ):
+        rows = slice(r * TREE, (r + 1) * TREE)
+        valid = pos < left[r, 0:1, :]
+        for g in range(KVH):
+            cols = slice(g * HD, (g + 1) * HD)
+            heads = slice(g * GROUP, (g + 1) * GROUP)
+            qh = q[heads, rows, :].reshape(GROUP * TREE, HD)
             s = lax.dot_general(k[r, :, cols], qh, nt, preferred_element_type=f32) * score_scale
-            valid = pos < cache_len[r]
             s = jnp.where(valid, s, floor_score)
             top = jnp.max(s, axis=0, keepdims=True)
             e = jnp.where(valid, jnp.exp(s - top), 0.0)
@@ -105,7 +119,7 @@
             lse = jnp.where(some, top + jnp.log(jnp.where(some, total, 1.0)), floor_score)
             p = (e * inv).astype(bf16)
             o = lax.dot_general(p, v[r, :, cols], tn, preferred_element_type=f32)
-            out[g * GROUP : (g + 1) * GROUP, rows, :] = o.astype(bf16).reshape(GROUP, TREE, HD)
+            out[heads, rows, :] = o.astype(bf16).reshape(GROUP, TREE, HD)
             turned = pltpu.roll(
                 jnp.broadcast_to(pltpu.roll(lse, (r + 1) * TREE, 1), (GROUP, HD)),
                 0,
@@ -113,8 +127,9 @@
                 stride=TREE,
                 stride_axis=0,
             )
-            packed = jnp.where(lane // TREE == r, turned, packed)
-        hi, mid, lo = three_parts(packed)
+            packed[g] = jnp.where(lane // TREE == r, turned, packed[g])
+    for g in range(KVH):
+        hi, mid, lo = three_parts(packed[g])
         first = jnp.where(lane < ROWS, hi, pltpu.roll(mid, ROWS, 1))
         for j in range(GROUP):
             i = GROUP - 1 - j
@@ -152,28 +167,33 @@
         h = h + got[c].astype(f32)
     h_ref[...] = h
     layer_ref[...] = h.astype(bf16)
-    sq = lax.dot_general(
-        jnp.ones((8, h.shape[1]), f32),
-        h * h,
-        (((1,), (1,)), ((), ())),
-        preferred_element_type=f32,
-        precision=lax.Precision.HIGHEST,
-    )
-    sq_ref[...] = jnp.broadcast_to(sq[0:1, :][None], sq_ref.shape)
+    sq = h * h
+    part = sq[:, :HD]
+    for c in range(HD, sq.shape[1], HD):
+        part = part + sq[:, c : c + HD]
+    row = jnp.sum(part.T, axis=0, keepdims=True)
+    row = jnp.concatenate([row, jnp.zeros((1, HD - ROWS), f32)], axis=1)
+    hi, mid, lo = three_parts(row)
+    sub = iota((STAT, HD), 0)
+    tile = jnp.where(sub == 0, hi, jnp.where(sub == 1, mid, jnp.where(sub == 2, lo, 0.0))).astype(bf16)
+    for c in range(sq_ref.shape[0]):
+        sq_ref[c] = tile
 
 
 def draft_kernel(got, h, gain, sel, out):
-    sq = got[...].reshape(got.shape[0], ROWS)
-    total = lax.dot_general(
-        sq,
-        jnp.ones((got.shape[0], h.shape[1]), f32),
-        (((0,), (0,)), ((), ())),
-        preferred_element_type=f32,
-        precision=lax.Precision.HIGHEST,
-    )
-    scale = lax.rsqrt(total / D + epsilon)
-    feat = (h[...] * scale * gain[...].astype(f32)).astype(bf16)
-    out[...] = jnp.dot(sel[...], feat, preferred_element_type=f32).astype(bf16)
+    tile = got[0].astype(f32)
+    for c in range(1, got.shape[0]):
+        tile = tile + got[c].astype(f32)
+    total = jnp.sum(tile, axis=0, keepdims=True)
+    scale = lax.rsqrt(jnp.broadcast_to(total / D, (HD, HD)).T[:ROWS, :] + epsilon)
+    for c in range(0, h.shape[1], HD):
+        cols = slice(c, c + HD)
+        feat = (h[:, cols] * scale * gain[:, cols].astype(f32)).astype(bf16)
+        out[:, cols] = jnp.dot(sel[...], feat, preferred_element_type=f32).astype(bf16)
+
+
+def params(mib):
+    return pltpu.CompilerParams(vmem_limit_bytes=mib * 2**20)
 
 
 def shape(dims, kind):
@@ -196,26 +216,42 @@
     count = lax.axis_size("tensor")
     rank = lax.axis_index("tensor").astype(jnp.int32).reshape(1)
     width = residual.shape[1]
-    q_all = to_all(jnp.broadcast_to(q_rows, (count, ROWS, HD)))
-    o_tree, lse_tree, sel = pl.pallas_call(
+    q_each = pl.pallas_call(
+        spread_kernel,
+        name="spread",
+        compiler_params=params(2),
+        out_shape=shape((count, ROWS, HD), bf16),
+        in_specs=[SM, VM],
+        out_specs=VM,
+    )(lax.axis_index("dp").astype(jnp.int32).reshape(1) % 2, q_rows)
+    q_all = to_all(q_each)
+    o_tree, lse_tree, sel, left = pl.pallas_call(
         tree_kernel,
         name="tree",
-        out_shape=(shape((ROWS, HD), f32), shape((8, ROWS), f32), shape((REQ * MAXACC, ROWS), bf16)),
-        in_specs=[SM, SM, VM, VM, VM, SM],
-        out_specs=(VM, VM, VM),
-        cost_estimate=pl.CostEstimate(flops=10**8, bytes_accessed=300000, transcendentals=10000),
-    )(rank, parents, q_rows, k_tree, v_tree, accepted_node)
+        compiler_params=params(6),
+        out_shape=(
+            shape((ROWS, HD), f32),
+            shape((8, ROWS), f32),
+            shape((REQ * MAXACC, ROWS), bf16),
+            shape((REQ, 8, HD), jnp.int32),
+        ),
+        in_specs=[SM, SM, SM, SM, VM, VM, VM, VM, VM],
+        out_specs=(VM, VM, VM, VM),
+        cost_estimate=pl.CostEstimate(flops=10**8, bytes_accessed=4 * 10**6, transcendentals=10000),
+    )(rank, parents, accepted_node, cache_len, q_rows, k_tree, v_tree, k_cache, v_cache)
     sent = pl.pallas_call(
         attend_kernel,
         name="attend",
+        compiler_params=params(10),
         out_shape=shape((HEADS, MSG, HD), bf16),
-        in_specs=[SM, SM, VM, VM, VM],
-        out_specs=VM,
-    )(rank, cache_len, q_all, k_cache, v_cache)
+        in_specs=[VM, VM, VM, VM],
+        out_specs=VM,
+    )(left, q_all, k_cache, v_cache)
     got = to_all(sent)
     terms = pl.pallas_call(
         project_kernel,
         name="project",
+        compiler_params=params(10),
         out_shape=shape((count, ROWS, width), bf16),
         in_specs=[VM, VM, VM, VM],
         out_specs=VM,
@@ -224,7 +260,8 @@
     h, layer_out, squares = pl.pallas_call(
         hidden_kernel,
         name="hidden",
-        out_shape=(shape((ROWS, width), f32), shape((ROWS, width), bf16), shape((count, 1, ROWS), f32)),
+        compiler_params=params(6),
+        out_shape=(shape((ROWS, width), f32), shape((ROWS, width), bf16), shape((count, STAT, HD), bf16)),
         in_specs=[VM, VM],
         out_specs=(VM, VM, VM),
     )(arrived, residual)
@@ -232,6 +269,7 @@
     draft = pl.pallas_call(
         draft_kernel,
         name="draft",
+        compiler_params=params(4),
         out_shape=shape((REQ * MAXACC, width), bf16),
         in_specs=[VM, VM, VM, VM],
         out_specs=VM,

time: 116 us -> 98.9 us (0.85); the launches traced: 114 us -> 98.3 us
  waiting for transfers between devices: 35.3 us -> 13.3 us
  blocking collectives: 33.2 us -> 42.9 us
  starting transfers between devices: 25.6 us -> 16.2 us
  Pallas kernels: 14.6 us -> 18.8 us
  local copies, waits for them, and re-layouts: 4.46 us -> 6.43 us
    all_to_all x3 -> x2, waiting for transfers between devices: 35.3 us -> 13.3 us  [to_all(): return lax.all_to_all(x, 'tensor', split_axis=0, concat_axis=0, tiled=True)]
    all_to_all x1 -> x2, blocking collectives: 33.2 us -> 42.9 us  [to_all(): return lax.all_to_all(x, 'tensor', split_axis=0, concat_axis=0, tiled=True)]
    all_to_all x3 -> x2, starting transfers between devices: 25.6 us -> 16.2 us  [to_all(): return lax.all_to_all(x, 'tensor', split_axis=0, concat_axis=0, tiled=True)]
    pallas_call x5 -> x6, Pallas kernels: 14.6 us -> 18.8 us  [the longest x1 12.9 us: on_device(): pl.pallas_call(spread_kernel, name='spread', compiler_params=params(2), o...]
    unnamed x8 -> x26, local copies, waits for them, and re-layouts: 2.25 us -> 6.42 us
    broadcast_in_dim x1 -> x0, local copies, waits for them, and re-layouts: 1.63 us -> none  [on_device(): q_all = to_all(jnp.broadcast_to(q_rows, (count, ROWS, HD)))]
  transfers between devices with their start and end apart: 3 -> 2, of which waited for: 3 -> 2; matrix products, arithmetic and copies ran while one was open for 1% -> 0% of each run, Pallas kernels for 2% -> 1%
where the time goes in v2:
time: 98.9 us; the launch traced here: 98.3 us
  blocking collectives  42.9 us (43%)
  Pallas kernels  18.8 us (19%)
  starting transfers between devices  16.2 us (16%)
  waiting for transfers between devices  13.3 us (13%)
  local copies, waits for them, and re-layouts  6.43 us (7%)
    all_to_all x2, blocking collectives, to_all(): return lax.all_to_all(x, 'tensor', split_axis=0, concat_axis=0, tiled=True)  42.9 us
    all_to_all x2, starting transfers between devices, to_all(): return lax.all_to_all(x, 'tensor', split_axis=0, concat_axis=0, tiled=True)  16.2 us
    all_to_all x2, waiting for transfers between devices, to_all(): return lax.all_to_all(x, 'tensor', split_axis=0, concat_axis=0, tiled=True)  13.3 us
    pallas_call x1, Pallas kernels, on_device(): pl.pallas_call(spread_kernel, name='spread', compiler_params=params(2), o...  12.9 us
    unnamed x26, local copies, waits for them, and re-layouts  6.42 us
  transfers between devices with their start and end apart: 2, of which 2 were waited for; matrix products, arithmetic and copies ran while one was open for 0% of the time, Pallas kernels for 1%

profile of v2, /device:TPU:1, one launch (start us, length us, event | category | flops | bytes accessed | tf_op | source)
XLA Modules:
  0.0 98.3 jit_solution(17777057119490806354)
XLA Ops:
  0.6 0.0 copy-start
  0.7 0.0 copy-start.4
  0.7 0.8 copy-done.4
  1.5 12.9 %spread.1 = bf16[32,64,128]{2,1,0:T(8,128)(2,1)} custom-call(s32[1]{0:T(128)S(6)} %select_n.7.late, bf16[64,128]{1,0:T(8,128)(2,1)S(1)} %copy-done.4), custom_call_target="tpu_custom_call" | custom-call | tf_op jit(solution)/shard_map/spread/pallas_call | solution.py:219
  14.3 10.5 %all-to-all-start = ((bf16[32,64,128]{2,1,0:T(8,128)(2,1)}), bf16[32,64,128]{2,1,0:T(8,128)(2,1)S(1)}, u32[]{:S(2)}, u32[]{:S(2)}) async-start(bf16[32,64,128]{2,1,0:T(8,128)(2,1)} %spread.1), calls=%async_computation | async-start | bytes 1048576 | tf_op jit(solution)/shard_map/all_to_all | solution.py:41
  24.8 0.0 copy-done
  24.8 0.0 copy-start.1
  24.9 1.2 %copy-done.1 = bf16[4,256,512]{2,1,0:T(8,128)(2,1)S(1)} copy-done((bf16[4,256,512]{2,1,0:T(8,128)(2,1)S(1)}, bf16[4,256,512]{2,1,0:T(8,128)(2,1)}, u32[]{:S(2)}) %copy-start.1) | copy-done | bytes 1048600
  26.1 0.0 copy-start.5
  26.1 0.7 copy-done.5
  26.8 0.0 copy-start.6
  26.8 0.8 copy-done.6
  27.6 0.0 copy-start.7
  27.6 0.8 copy-done.7
  28.5 0.0 copy-start.9
  28.5 0.7 copy-done.9
  29.1 0.0 copy-start.10
  29.2 0.7 copy-done.10
  29.8 0.0 copy-start.11
  29.8 0.7 copy-done.11
  30.5 0.0 copy-start.2
  30.5 1.3 %tree.1 = (f32[64,128]{1,0:T(8,128)S(1)}, f32[8,64]{1,0:T(8,128)S(1)}, bf16[32,64]{1,0:T(8,128)(2,1)S(1)}, s32[4,8,128]{2,1,0:T(8,128)S(1)}) custom-call(s32[1]{0:T(128)} %bitcast.rank, s32[4,16]{1,0:T(4,128)S(1)} %copy-done.9, s32[4]{0:T(128)S(1)} %copy-done.10, s32[4]{0:T(128)S(1)} %copy-done.11, bf16[64,128]{1,0:T(8,128)(2,1)S(1)} %copy-done.5, ...), custom_call_target="tpu_custom_call" | custom-call | flops 100000000 | bytes 4000000 | tf_op jit(solution)/shard_map/tree/pallas_call | solution.py:228
  31.8 4.4 %all-to-all-done.q = bf16[32,64,128]{2,1,0:T(8,128)(2,1)S(1)} async-done(((bf16[32,64,128]{2,1,0:T(8,128)(2,1)}), bf16[32,64,128]{2,1,0:T(8,128)(2,1)S(1)}, u32[]{:S(2)}, u32[]{:S(2)}) %all-to-all-start) | async-done | bytes 524320 | tf_op jit(solution)/shard_map/all_to_all | solution.py:41
  36.2 0.0 copy-done.2
  36.2 0.0 copy-start.3
  36.2 1.8 %attend.1 = bf16[32,72,128]{2,1,0:T(8,128)(2,1)S(1)} custom-call(s32[4,8,128]{2,1,0:T(8,128)S(1)} %get-tuple-element.9.left, bf16[32,64,128]{2,1,0:T(8,128)(2,1)S(1)} %all-to-all-done.q, bf16[4,256,512]{2,1,0:T(8,128)(2,1)S(1)} %copy-done, bf16[4,256,512]{2,1,0:T(8,128)(2,1)S(1)} %copy-done.2), custom_call_target="tpu_custom_call" | custom-call | tf_op jit(solution)/shard_map/attend/pallas_call | solution.py:242
  38.0 18.0 %all_to_all.20.got = bf16[32,72,128]{2,1,0:T(8,128)(2,1)S(1)} all-to-all(bf16[32,72,128]{2,1,0:T(8,128)(2,1)S(1)} %attend.1), channel_id=1, replica_groups=mesh['dp'=16,'tensor'=32] {'tensor'}, dimensions={0} | all-to-all | bytes 1179648 | tf_op jit(solution)/shard_map/all_to_all | solution.py:41
  56.0 0.0 copy-done.3
  56.0 0.0 copy-start.8
  56.0 1.1 %project.1 = bf16[32,64,256]{2,1,0:T(8,128)(2,1)S(1)} custom-call(bf16[32,72,128]{2,1,0:T(8,128)(2,1)S(1)} %all_to_all.20.got, f32[64,128]{1,0:T(8,128)S(1)} %get-tuple-element.10.o_tree, f32[8,64]{1,0:T(8,128)S(1)} %get-tuple-element.11.lse_tree, bf16[128,8192]{1,0:T(8,128)(2,1)S(1)} %copy-done.3), custom_call_target="tpu_custom_call" | custom-call | tf_op jit(solution)/shard_map/project/pallas_call | solution.py:251
  57.1 0.0 copy-start.12
  57.1 24.9 %all_to_all.21.got = bf16[32,64,256]{2,1,0:T(8,128)(2,1)S(1)} all-to-all(bf16[32,64,256]{2,1,0:T(8,128)(2,1)S(1)} %project.1), channel_id=1, replica_groups=mesh['dp'=16,'tensor'=32] {'tensor'}, dimensions={0} | all-to-all | bytes 2097152 | tf_op jit(solution)/shard_map/all_to_all | solution.py:41
  82.0 0.0 copy-done.8
  82.0 0.9 hidden.1
  82.9 5.7 %all-to-all-start.3 = ((bf16[32,8,128]{2,1,0:T(8,128)(2,1)}), bf16[32,8,128]{2,1,0:T(8,128)(2,1)S(1)}, u32[]{:S(2)}, u32[]{:S(2)}) async-start(bf16[32,8,128]{2,1,0:T(8,128)(2,1)} %get-tuple-element.13), calls=%async_computation.3 | async-start | bytes 131072 | tf_op jit(solution)/shard_map/all_to_all | solution.py:41
  88.6 0.0 copy-done.12
  88.6 8.8 %all-to-all-done.3.got = bf16[32,8,128]{2,1,0:T(8,128)(2,1)S(1)} async-done(((bf16[32,8,128]{2,1,0:T(8,128)(2,1)}), bf16[32,8,128]{2,1,0:T(8,128)(2,1)S(1)}, u32[]{:S(2)}, u32[]{:S(2)}) %all-to-all-start.3) | async-done | bytes 65568 | tf_op jit(solution)/shard_map/all_to_all | solution.py:41
  97.4 0.9 draft.1
  (1 shorter events, 0.0 us)
Async XLA Ops:
  0.6 24.2 %copy-start = (bf16[4,256,512]{2,1,0:T(8,128)(2,1)S(1)}, bf16[4,256,512]{2,1,0:T(8,128)(2,1)}, u32[]{:S(2)}) copy-start(bf16[4,256,512]{2,1,0:T(8,128)(2,1)} %k.3) | copy-start | bytes 3145732
  0.7 0.8 copy-start.4
  14.3 21.9 %all-to-all-start = ((bf16[32,64,128]{2,1,0:T(8,128)(2,1)}), bf16[32,64,128]{2,1,0:T(8,128)(2,1)S(1)}, u32[]{:S(2)}, u32[]{:S(2)}) async-start(bf16[32,64,128]{2,1,0:T(8,128)(2,1)} %spread.1), calls=%async_computation | async-start | bytes 1048576 | tf_op jit(solution)/shard_map/all_to_all | solution.py:41
  24.8 1.2 %copy-start.1 = (bf16[4,256,512]{2,1,0:T(8,128)(2,1)S(1)}, bf16[4,256,512]{2,1,0:T(8,128)(2,1)}, u32[]{:S(2)}) copy-start(bf16[4,256,512]{2,1,0:T(8,128)(2,1)} %v.3) | copy-start | bytes 3145732
  26.1 0.7 copy-start.5
  26.8 0.8 copy-start.6
  27.6 0.8 copy-start.7
  28.5 0.7 copy-start.9
  29.1 0.7 copy-start.10
  29.8 0.7 copy-start.11
  30.5 5.8 %copy-start.2 = (bf16[4,256,512]{2,1,0:T(8,128)(2,1)S(1)}, bf16[4,256,512]{2,1,0:T(8,128)(2,1)}, u32[]{:S(2)}) copy-start(bf16[4,256,512]{2,1,0:T(8,128)(2,1)} %v.3) | copy-start | bytes 3145732
  36.2 19.8 %copy-start.3 = (bf16[128,8192]{1,0:T(8,128)(2,1)S(1)}, bf16[128,8192]{1,0:T(8,128)(2,1)}, u32[]{:S(2)}) copy-start(bf16[128,8192]{1,0:T(8,128)(2,1)} %wo.1) | copy-start | bytes 6291460
  56.0 26.0 %copy-start.8 = (bf16[64,256]{1,0:T(8,128)(2,1)S(1)}, bf16[64,256]{1,0:T(8,128)(2,1)}, u32[]{:S(2)}) copy-start(bf16[64,256]{1,0:T(8,128)(2,1)} %residual.1) | copy-start | bytes 98308
  57.1 31.5 %copy-start.12 = (bf16[256]{0:T(256)(128)(2,1)S(1)}, bf16[256]{0:T(256)(128)(2,1)}, u32[]{:S(2)}) copy-start(bf16[256]{0:T(256)(128)(2,1)} %param.18) | copy-start | bytes 1540
  82.9 14.5 %all-to-all-start.3 = ((bf16[32,8,128]{2,1,0:T(8,128)(2,1)}), bf16[32,8,128]{2,1,0:T(8,128)(2,1)S(1)}, u32[]{:S(2)}, u32[]{:S(2)}) async-start(bf16[32,8,128]{2,1,0:T(8,128)(2,1)} %get-tuple-element.13), calls=%async_computation.3 | async-start | bytes 131072 | tf_op jit(solution)/shard_map/all_to_all | solution.py:41

commit v3 on v2

--- a/solution.py
+++ b/solution.py
@@ -23,8 +23,9 @@
 f32 = jnp.float32
 bf16 = jnp.bfloat16
 VM = pl.BlockSpec(memory_space=pltpu.VMEM)
+HB = pl.BlockSpec(memory_space=pltpu.HBM)
 SM = pl.BlockSpec(memory_space=pltpu.SMEM)
-STAGGER = 12000
+STAGGER = 10000
 
 
 def iota(shape, dim):
@@ -41,18 +42,33 @@
     return lax.all_to_all(x, "tensor", split_axis=0, concat_axis=0, tiled=True)
 
 
-def spread_kernel(late, q, out):
+def spread_kernel(late, q, out, here, sems):
+    fetch = pltpu.make_async_copy(q, here, sems.at[0])
+    fetch.start()
+
     @pl.when(late[0] > 0)
     def _():
         pl.delay(STAGGER)
 
-    for d in range(out.shape[0]):
-        out[d] = q[...]
+    fetch.wait()
+    copies = [pltpu.make_async_copy(here, out.at[d], sems.at[d]) for d in range(out.shape[0])]
+    for copy in copies:
+        copy.start()
+    for copy in copies:
+        copy.wait()
+
+
+def across(x, groups):
+    return lax.all_to_all(
+        x, "tensor", split_axis=0, concat_axis=0, axis_index_groups=groups, tiled=True
+    )
 
 
 def tree_kernel(
-    rank, parents, acc_node, cache_len, q, kt, vt, k, v, o_ref, lse_ref, sel_ref, left_ref
+    rank, parents, acc_node, cache_len, q, kt, vt, k, v, gain,
+    o_ref, lse_ref, sel_ref, left_ref, gain_ref,
 ):
+    gain_ref[...] = jnp.broadcast_to(gain[...].astype(f32), gain_ref.shape)
     for r in range(REQ):
         left_ref[r] = jnp.full((8, HD), cache_len[r] - rank[0] * k.shape[1], jnp.int32)
     row = iota((ROWS, ROWS), 0)
@@ -161,6 +177,14 @@
         out[d] = part.astype(bf16)
 
 
+def join_kernel(got, out):
+    for d in range(out.shape[0]):
+        total = got[0, d].astype(f32)
+        for c in range(1, got.shape[0]):
+            total = total + got[c, d].astype(f32)
+        out[d] = total.astype(bf16)
+
+
 def hidden_kernel(got, residual, h_ref, layer_ref, sq_ref):
     h = residual[...].astype(f32)
     for c in range(got.shape[0]):
@@ -188,7 +212,7 @@
     scale = lax.rsqrt(jnp.broadcast_to(total / D, (HD, HD)).T[:ROWS, :] + epsilon)
     for c in range(0, h.shape[1], HD):
         cols = slice(c, c + HD)
-        feat = (h[:, cols] * scale * gain[:, cols].astype(f32)).astype(bf16)
+        feat = (h[:, cols] * scale * gain[0:1, cols]).astype(bf16)
         out[:, cols] = jnp.dot(sel[...], feat, preferred_element_type=f32).astype(bf16)
 
 
@@ -219,13 +243,14 @@
     q_each = pl.pallas_call(
         spread_kernel,
         name="spread",
-        compiler_params=params(2),
+        compiler_params=params(60),
         out_shape=shape((count, ROWS, HD), bf16),
-        in_specs=[SM, VM],
-        out_specs=VM,
+        in_specs=[SM, HB],
+        out_specs=HB,
+        scratch_shapes=[pltpu.VMEM((ROWS, HD), bf16), pltpu.SemaphoreType.DMA((count,))],
     )(lax.axis_index("dp").astype(jnp.int32).reshape(1) % 2, q_rows)
     q_all = to_all(q_each)
-    o_tree, lse_tree, sel, left = pl.pallas_call(
+    o_tree, lse_tree, sel, left, gains = pl.pallas_call(
         tree_kernel,
         name="tree",
         compiler_params=params(6),
@@ -234,11 +259,15 @@
             shape((8, ROWS), f32),
             shape((REQ * MAXACC, ROWS), bf16),
             shape((REQ, 8, HD), jnp.int32),
+            shape((8, width), f32),
         ),
-        in_specs=[SM, SM, SM, SM, VM, VM, VM, VM, VM],
-        out_specs=(VM, VM, VM, VM),
+        in_specs=[SM, SM, SM, SM, VM, VM, VM, VM, VM, VM],
+        out_specs=(VM, VM, VM, VM, VM),
         cost_estimate=pl.CostEstimate(flops=10**8, bytes_accessed=4 * 10**6, transcendentals=10000),
-    )(rank, parents, accepted_node, cache_len, q_rows, k_tree, v_tree, k_cache, v_cache)
+    )(
+        rank, parents, accepted_node, cache_len, q_rows, k_tree, v_tree, k_cache, v_cache,
+        gain.reshape(1, width),
+    )
     sent = pl.pallas_call(
         attend_kernel,
         name="attend",
@@ -256,7 +285,19 @@
         in_specs=[VM, VM, VM, VM],
         out_specs=VM,
     )(got, o_tree, lse_tree, wo_rows)
-    arrived = to_all(terms)
+    lines, size = 4, count // 4
+    along_x = [[x * size + y for x in range(lines)] for y in range(size)]
+    along_y = [[x * size + y for y in range(size)] for x in range(lines)]
+    part = across(terms.reshape(lines, size * ROWS, width), along_x)
+    joined = pl.pallas_call(
+        join_kernel,
+        name="join",
+        compiler_params=params(6),
+        out_shape=shape((size, ROWS, width), bf16),
+        in_specs=[VM],
+        out_specs=VM,
+    )(part.reshape(lines, size, ROWS, width))
+    arrived = across(joined, along_y)
     h, layer_out, squares = pl.pallas_call(
         hidden_kernel,
         name="hidden",
@@ -273,7 +314,7 @@
         out_shape=shape((REQ * MAXACC, width), bf16),
         in_specs=[VM, VM, VM, VM],
         out_specs=VM,
-    )(totals, h, gain.reshape(1, width), sel)
+    )(totals, h, gains, sel)
     return (layer_out, draft.reshape(REQ, MAXACC, width))
 
 

time: 98.9 us -> 94 us (0.950)
  blocking collectives: 42.9 us -> 55.2 us
  waiting for transfers between devices: 13.3 us -> 3.77 us
  starting transfers between devices: 16.2 us -> 10.5 us
  Pallas kernels: 18.8 us -> 16.9 us
    all_to_all x0 -> x2, blocking collectives: none -> 24.2 us  [across(): lax.all_to_all(x, 'tensor', split_axis=0, concat_axis=0, axis_index_group...]
    all_to_all x2, blocking collectives: 42.9 us -> 31 us  [to_all(): return lax.all_to_all(x, 'tensor', split_axis=0, concat_axis=0, tiled=True)]
    all_to_all x2 -> x1, waiting for transfers between devices: 13.3 us -> 3.77 us  [to_all(): return lax.all_to_all(x, 'tensor', split_axis=0, concat_axis=0, tiled=True)]
    all_to_all x2 -> x1, starting transfers between devices: 16.2 us -> 10.5 us  [to_all(): return lax.all_to_all(x, 'tensor', split_axis=0, concat_axis=0, tiled=True)]
    pallas_call x1 -> x2, Pallas kernels: 12.9 us -> 11.2 us  [the longest x1 11.1 us: on_device(): pl.pallas_call(spread_kernel, name='spread', compiler_params=params(60),...]
    unnamed x26 -> x22, local copies, waits for them, and re-layouts: 6.42 us -> 5.63 us
  transfers between devices with their start and end apart: 2 -> 1, of which waited for: 2 -> 1; matrix products, arithmetic and copies ran while one was open for 0% -> 1% of each run, Pallas kernels for 1% -> 1%
where the time goes in v3:
time: 94 us; the launch traced here: 93.4 us
  blocking collectives  55.2 us (59%)
  Pallas kernels  16.9 us (18%)
  starting transfers between devices  10.5 us (11%)
  local copies, waits for them, and re-layouts  6.29 us (7%)
  waiting for transfers between devices  3.77 us (4%)
    all_to_all x2, blocking collectives, to_all(): return lax.all_to_all(x, 'tensor', split_axis=0, concat_axis=0, tiled=True)  31 us
    all_to_all x2, blocking collectives, across(): lax.all_to_all(x, 'tensor', split_axis=0, concat_axis=0, axis_index_group...  24.2 us
    pallas_call x1, Pallas kernels, on_device(): pl.pallas_call(spread_kernel, name='spread', compiler_params=params(60),...  11.1 us
    all_to_all x1, starting transfers between devices, to_all(): return lax.all_to_all(x, 'tensor', split_axis=0, concat_axis=0, tiled=True)  10.5 us
    unnamed x22, local copies, waits for them, and re-layouts  5.63 us
    all_to_all x1, waiting for transfers between devices, to_all(): return lax.all_to_all(x, 'tensor', split_axis=0, concat_axis=0, tiled=True)  3.77 us
  transfers between devices with their start and end apart: 1, of which 1 were waited for; matrix products, arithmetic and copies ran while one was open for 1% of the time, Pallas kernels for 1%

profile of v3, /device:TPU:1, one launch (start us, length us, event | category | flops | bytes accessed | tf_op | source)
XLA Modules:
  0.0 93.4 jit_solution(9723126000937789787)
XLA Ops:
  0.6 0.0 copy-start
  0.7 11.1 %spread.1 = bf16[32,64,128]{2,1,0:T(8,128)(2,1)} custom-call(s32[1]{0:T(128)S(6)} %select_n.7.late, bf16[64,128]{1,0:T(8,128)(2,1)} %q.3), custom_call_target="tpu_custom_call" | custom-call | tf_op jit(solution)/shard_map/spread/pallas_call | solution.py:243
  11.7 10.5 %all-to-all-start = ((bf16[32,64,128]{2,1,0:T(8,128)(2,1)}), bf16[32,64,128]{2,1,0:T(8,128)(2,1)S(1)}, u32[]{:S(2)}, u32[]{:S(2)}) async-start(bf16[32,64,128]{2,1,0:T(8,128)(2,1)} %spread.1), calls=%async_computation | async-start | bytes 1048576 | tf_op jit(solution)/shard_map/all_to_all | solution.py:42
  22.2 0.7 reshape.25.gain
  22.9 0.0 copy-done
  22.9 0.0 copy-start.1
  22.9 1.2 %copy-done.1 = bf16[4,256,512]{2,1,0:T(8,128)(2,1)S(1)} copy-done((bf16[4,256,512]{2,1,0:T(8,128)(2,1)S(1)}, bf16[4,256,512]{2,1,0:T(8,128)(2,1)}, u32[]{:S(2)}) %copy-start.1) | copy-done | bytes 1048600
  24.1 0.0 copy-start.4
  24.1 0.7 copy-done.4
  24.9 0.0 copy-start.5
  24.9 0.8 copy-done.5
  25.7 0.0 copy-start.6
  25.7 0.8 copy-done.6
  26.5 0.0 copy-start.8
  26.5 0.7 copy-done.8
  27.2 0.0 copy-start.9
  27.2 0.7 copy-done.9
  27.9 0.0 copy-start.10
  27.9 0.7 copy-done.10
  28.5 0.0 copy-start.2
  28.5 1.3 %tree.1 = (f32[64,128]{1,0:T(8,128)S(1)}, f32[8,64]{1,0:T(8,128)S(1)}, bf16[32,64]{1,0:T(8,128)(2,1)S(1)}, s32[4,8,128]{2,1,0:T(8,128)S(1)}, f32[8,256]{1,0:T(8,128)S(1)}) custom-call(s32[1]{0:T(128)} %bitcast.rank, s32[4,16]{1,0:T(4,128)S(1)} %copy-done.8, s32[4]{0:T(128)S(1)} %copy-done.9, s32[4]{0:T(128)S(1)} %copy-done.10, ...), custom_call_target="tpu_custom_call" | custom-call | flops 100000000 | bytes 4000000 | tf_op jit(solution)/shard_map/tree/pallas_call | solution.py:253
  29.9 3.8 %all-to-all-done.q = bf16[32,64,128]{2,1,0:T(8,128)(2,1)S(1)} async-done(((bf16[32,64,128]{2,1,0:T(8,128)(2,1)}), bf16[32,64,128]{2,1,0:T(8,128)(2,1)S(1)}, u32[]{:S(2)}, u32[]{:S(2)}) %all-to-all-start) | async-done | bytes 524320 | tf_op jit(solution)/shard_map/all_to_all | solution.py:42
  33.6 0.0 copy-done.2
  33.6 0.0 copy-start.3
  33.6 1.8 %attend.1 = bf16[32,72,128]{2,1,0:T(8,128)(2,1)S(1)} custom-call(s32[4,8,128]{2,1,0:T(8,128)S(1)} %get-tuple-element.10.left, bf16[32,64,128]{2,1,0:T(8,128)(2,1)S(1)} %all-to-all-done.q, bf16[4,256,512]{2,1,0:T(8,128)(2,1)S(1)} %copy-done, bf16[4,256,512]{2,1,0:T(8,128)(2,1)S(1)} %copy-done.2), custom_call_target="tpu_custom_call" | custom-call | tf_op jit(solution)/shard_map/attend/pallas_call | solution.py:271
  35.5 19.1 %all_to_all.25.got = bf16[32,72,128]{2,1,0:T(8,128)(2,1)S(1)} all-to-all(bf16[32,72,128]{2,1,0:T(8,128)(2,1)S(1)} %attend.1), channel_id=1, replica_groups=mesh['dp'=16,'tensor'=32] {'tensor'}, dimensions={0} | all-to-all | bytes 1179648 | tf_op jit(solution)/shard_map/all_to_all | solution.py:42
  54.6 0.0 copy-done.3
  54.6 1.1 %project.1 = bf16[32,64,256]{2,1,0:T(8,128)(2,1)S(1)} custom-call(bf16[32,72,128]{2,1,0:T(8,128)(2,1)S(1)} %all_to_all.25.got, f32[64,128]{1,0:T(8,128)S(1)} %get-tuple-element.11.o_tree, f32[8,64]{1,0:T(8,128)S(1)} %get-tuple-element.12.lse_tree, bf16[128,8192]{1,0:T(8,128)(2,1)S(1)} %copy-done.3), custom_call_target="tpu_custom_call" | custom-call | tf_op jit(solution)/shard_map/project/pallas_call | solution.py:280
  55.7 0.0 copy-start.7
  55.7 12.2 %all_to_all.26 = bf16[4,512,256]{2,1,0:T(8,128)(2,1)S(1)} all-to-all(bf16[4,512,256]{2,1,0:T(8,128)(2,1)S(1)} %bitcast.5), channel_id=1, replica_groups={{0,8,16,24},{1,9,17,25},{2,10,18,26},{3,11,19,27},{4,12,20,28},{5,13,21..., dimensions={0} | all-to-all | bytes 2097152 | tf_op jit(solution)/shard_map/all_to_all | solution.py:62
  67.9 0.1 join.1
  68.0 12.0 %all_to_all.27.got = bf16[8,64,256]{2,1,0:T(8,128)(2,1)S(1)} all-to-all(bf16[8,64,256]{2,1,0:T(8,128)(2,1)S(1)} %join.1), channel_id=1, replica_groups={{0,1,2,3,4,5,6,7},{8,9,10,11,12,13,14,15},{16,17,18,19,20,21,22,23},{24..., dimensions={0} | all-to-all | bytes 524288 | tf_op jit(solution)/shard_map/all_to_all | solution.py:62
  80.0 0.0 copy-done.7
  80.0 0.7 hidden.1
  80.7 11.8 %all_to_all.28.got = bf16[32,8,128]{2,1,0:T(8,128)(2,1)S(1)} all-to-all(bf16[32,8,128]{2,1,0:T(8,128)(2,1)S(1)} %get-tuple-element.14), channel_id=1, replica_groups=mesh['dp'=16,'tensor'=32] {'tensor'}, dimensions={0} | all-to-all | bytes 131072 | tf_op jit(solution)/shard_map/all_to_all | solution.py:42
  92.5 0.9 draft.1
Async XLA Ops:
  0.6 22.3 %copy-start = (bf16[4,256,512]{2,1,0:T(8,128)(2,1)S(1)}, bf16[4,256,512]{2,1,0:T(8,128)(2,1)}, u32[]{:S(2)}) copy-start(bf16[4,256,512]{2,1,0:T(8,128)(2,1)} %k.3) | copy-start | bytes 3145732
  11.7 21.9 %all-to-all-start = ((bf16[32,64,128]{2,1,0:T(8,128)(2,1)}), bf16[32,64,128]{2,1,0:T(8,128)(2,1)S(1)}, u32[]{:S(2)}, u32[]{:S(2)}) async-start(bf16[32,64,128]{2,1,0:T(8,128)(2,1)} %spread.1), calls=%async_computation | async-start | bytes 1048576 | tf_op jit(solution)/shard_map/all_to_all | solution.py:42
  22.9 1.2 %copy-start.1 = (bf16[4,256,512]{2,1,0:T(8,128)(2,1)S(1)}, bf16[4,256,512]{2,1,0:T(8,128)(2,1)}, u32[]{:S(2)}) copy-start(bf16[4,256,512]{2,1,0:T(8,128)(2,1)} %v.3) | copy-start | bytes 3145732
  24.1 0.7 copy-start.4
  24.9 0.8 copy-start.5
  25.7 0.8 copy-start.6
  26.5 0.7 copy-start.8
  27.2 0.7 copy-start.9
  27.9 0.7 copy-start.10
  28.5 5.1 %copy-start.2 = (bf16[4,256,512]{2,1,0:T(8,128)(2,1)S(1)}, bf16[4,256,512]{2,1,0:T(8,128)(2,1)}, u32[]{:S(2)}) copy-start(bf16[4,256,512]{2,1,0:T(8,128)(2,1)} %v.3) | copy-start | bytes 3145732
  33.6 21.0 %copy-start.3 = (bf16[128,8192]{1,0:T(8,128)(2,1)S(1)}, bf16[128,8192]{1,0:T(8,128)(2,1)}, u32[]{:S(2)}) copy-start(bf16[128,8192]{1,0:T(8,128)(2,1)} %wo.1) | copy-start | bytes 6291460
  55.7 24.3 %copy-start.7 = (bf16[64,256]{1,0:T(8,128)(2,1)S(1)}, bf16[64,256]{1,0:T(8,128)(2,1)}, u32[]{:S(2)}) copy-start(bf16[64,256]{1,0:T(8,128)(2,1)} %residual.1) | copy-start | bytes 98308

commit v4 on v3

--- a/solution.py
+++ b/solution.py
@@ -23,9 +23,8 @@
 f32 = jnp.float32
 bf16 = jnp.bfloat16
 VM = pl.BlockSpec(memory_space=pltpu.VMEM)
-HB = pl.BlockSpec(memory_space=pltpu.HBM)
 SM = pl.BlockSpec(memory_space=pltpu.SMEM)
-STAGGER = 10000
+STAGGER = 9800
 
 
 def iota(shape, dim):
@@ -42,20 +41,13 @@
     return lax.all_to_all(x, "tensor", split_axis=0, concat_axis=0, tiled=True)
 
 
-def spread_kernel(late, q, out, here, sems):
-    fetch = pltpu.make_async_copy(q, here, sems.at[0])
-    fetch.start()
-
+def spread_kernel(late, q, out):
     @pl.when(late[0] > 0)
     def _():
         pl.delay(STAGGER)
 
-    fetch.wait()
-    copies = [pltpu.make_async_copy(here, out.at[d], sems.at[d]) for d in range(out.shape[0])]
-    for copy in copies:
-        copy.start()
-    for copy in copies:
-        copy.wait()
+    for d in range(out.shape[0]):
+        out[d] = q[...]
 
 
 def across(x, groups):
@@ -128,11 +120,11 @@
             s = lax.dot_general(k[r, :, cols], qh, nt, preferred_element_type=f32) * score_scale
             s = jnp.where(valid, s, floor_score)
             top = jnp.max(s, axis=0, keepdims=True)
-            e = jnp.where(valid, jnp.exp(s - top), 0.0)
+            e = jnp.exp(s - top)
             total = jnp.sum(e, axis=0, keepdims=True)
-            some = total > 0.0
-            inv = jnp.where(some, 1.0 / jnp.where(some, total, 1.0), 0.0)
-            lse = jnp.where(some, top + jnp.log(jnp.where(some, total, 1.0)), floor_score)
+            some = left[r, 0:1, :] > 0
+            inv = jnp.where(some, 1.0 / total, 0.0)
+            lse = jnp.where(some, top + jnp.log(total), floor_score)
             p = (e * inv).astype(bf16)
             o = lax.dot_general(p, v[r, :, cols], tn, preferred_element_type=f32)
             out[heads, rows, :] = o.astype(bf16).reshape(GROUP, TREE, HD)
@@ -243,11 +235,10 @@
     q_each = pl.pallas_call(
         spread_kernel,
         name="spread",
-        compiler_params=params(60),
+        compiler_params=params(2),
         out_shape=shape((count, ROWS, HD), bf16),
-        in_specs=[SM, HB],
-        out_specs=HB,
-        scratch_shapes=[pltpu.VMEM((ROWS, HD), bf16), pltpu.SemaphoreType.DMA((count,))],
+        in_specs=[SM, VM],
+        out_specs=VM,
     )(lax.axis_index("dp").astype(jnp.int32).reshape(1) % 2, q_rows)
     q_all = to_all(q_each)
     o_tree, lse_tree, sel, left, gains = pl.pallas_call(

time: 94 us -> 93.8 us (level)
    all_to_all x2, blocking collectives: 31 us -> 29.4 us  [to_all(): return lax.all_to_all(x, 'tensor', split_axis=0, concat_axis=0, tiled=True)]
    all_to_all x2, blocking collectives: 24.2 us -> 25.3 us  [across(): lax.all_to_all(x, 'tensor', split_axis=0, concat_axis=0, axis_index_group...]
    unnamed x22 -> x24, local copies, waits for them, and re-layouts: 5.63 us -> 6.43 us
where the time goes in v4:
time: 93.8 us; the launch traced here: 93.1 us
  blocking collectives  54.7 us (58%)
  Pallas kernels  16.4 us (17%)
  starting transfers between devices  10.5 us (11%)
  local copies, waits for them, and re-layouts  7.09 us (8%)
  waiting for transfers between devices  3.77 us (4%)
    all_to_all x2, blocking collectives, to_all(): return lax.all_to_all(x, 'tensor', split_axis=0, concat_axis=0, tiled=True)  29.4 us
    all_to_all x2, blocking collectives, across(): lax.all_to_all(x, 'tensor', split_axis=0, concat_axis=0, axis_index_group...  25.3 us
    pallas_call x1, Pallas kernels, on_device(): pl.pallas_call(spread_kernel, name='spread', compiler_params=params(2), o...  10.7 us
    all_to_all x1, starting transfers between devices, to_all(): return lax.all_to_all(x, 'tensor', split_axis=0, concat_axis=0, tiled=True)  10.5 us
    unnamed x24, local copies, waits for them, and re-layouts  6.43 us
    all_to_all x1, waiting for transfers between devices, to_all(): return lax.all_to_all(x, 'tensor', split_axis=0, concat_axis=0, tiled=True)  3.77 us
  transfers between devices with their start and end apart: 1, of which 1 were waited for; matrix products, arithmetic and copies ran while one was open for 1% of the time, Pallas kernels for 1%

profile of v4, /device:TPU:1, one launch (start us, length us, event | category | flops | bytes accessed | tf_op | source)
XLA Modules:
  0.0 93.1 jit_solution(13627971922545441098)
XLA Ops:
  0.6 0.0 copy-start
  0.7 0.0 copy-start.4
  0.7 0.8 copy-done.4
  1.5 10.7 %spread.1 = bf16[32,64,128]{2,1,0:T(8,128)(2,1)} custom-call(s32[1]{0:T(128)S(6)} %select_n.7.late, bf16[64,128]{1,0:T(8,128)(2,1)S(1)} %copy-done.4), custom_call_target="tpu_custom_call" | custom-call | tf_op jit(solution)/shard_map/spread/pallas_call | solution.py:235
  12.1 10.5 %all-to-all-start = ((bf16[32,64,128]{2,1,0:T(8,128)(2,1)}), bf16[32,64,128]{2,1,0:T(8,128)(2,1)S(1)}, u32[]{:S(2)}, u32[]{:S(2)}) async-start(bf16[32,64,128]{2,1,0:T(8,128)(2,1)} %spread.1), calls=%async_computation | async-start | bytes 1048576 | tf_op jit(solution)/shard_map/all_to_all | solution.py:41
  22.6 0.7 reshape.25.gain
  23.3 0.0 copy-done
  23.3 0.0 copy-start.1
  23.3 1.2 %copy-done.1 = bf16[4,256,512]{2,1,0:T(8,128)(2,1)S(1)} copy-done((bf16[4,256,512]{2,1,0:T(8,128)(2,1)S(1)}, bf16[4,256,512]{2,1,0:T(8,128)(2,1)}, u32[]{:S(2)}) %copy-start.1) | copy-done | bytes 1048600
  24.5 0.0 copy-start.5
  24.5 0.7 copy-done.5
  25.2 0.0 copy-start.6
  25.2 0.8 copy-done.6
  26.1 0.0 copy-start.7
  26.1 0.8 copy-done.7
  26.9 0.0 copy-start.9
  26.9 0.7 copy-done.9
  27.6 0.0 copy-start.10
  27.6 0.7 copy-done.10
  28.2 0.0 copy-start.11
  28.2 0.7 copy-done.11
  28.9 0.0 copy-start.2
  28.9 1.3 %tree.1 = (f32[64,128]{1,0:T(8,128)S(1)}, f32[8,64]{1,0:T(8,128)S(1)}, bf16[32,64]{1,0:T(8,128)(2,1)S(1)}, s32[4,8,128]{2,1,0:T(8,128)S(1)}, f32[8,256]{1,0:T(8,128)S(1)}) custom-call(s32[1]{0:T(128)} %bitcast.rank, s32[4,16]{1,0:T(4,128)S(1)} %copy-done.9, s32[4]{0:T(128)S(1)} %copy-done.10, s32[4]{0:T(128)S(1)} %copy-done.11, ...), custom_call_target="tpu_custom_call" | custom-call | flops 100000000 | bytes 4000000 | tf_op jit(solution)/shard_map/tree/pallas_call | solution.py:244
  30.2 3.8 %all-to-all-done.q = bf16[32,64,128]{2,1,0:T(8,128)(2,1)S(1)} async-done(((bf16[32,64,128]{2,1,0:T(8,128)(2,1)}), bf16[32,64,128]{2,1,0:T(8,128)(2,1)S(1)}, u32[]{:S(2)}, u32[]{:S(2)}) %all-to-all-start) | async-done | bytes 524320 | tf_op jit(solution)/shard_map/all_to_all | solution.py:41
  34.0 0.0 copy-done.2
  34.0 0.0 copy-start.3
  34.0 1.7 %attend.1 = bf16[32,72,128]{2,1,0:T(8,128)(2,1)S(1)} custom-call(s32[4,8,128]{2,1,0:T(8,128)S(1)} %get-tuple-element.10.left, bf16[32,64,128]{2,1,0:T(8,128)(2,1)S(1)} %all-to-all-done.q, bf16[4,256,512]{2,1,0:T(8,128)(2,1)S(1)} %copy-done, bf16[4,256,512]{2,1,0:T(8,128)(2,1)S(1)} %copy-done.2), custom_call_target="tpu_custom_call" | custom-call | tf_op jit(solution)/shard_map/attend/pallas_call | solution.py:262
  35.7 17.6 %all_to_all.25.got = bf16[32,72,128]{2,1,0:T(8,128)(2,1)S(1)} all-to-all(bf16[32,72,128]{2,1,0:T(8,128)(2,1)S(1)} %attend.1), channel_id=1, replica_groups=mesh['dp'=16,'tensor'=32] {'tensor'}, dimensions={0} | all-to-all | bytes 1179648 | tf_op jit(solution)/shard_map/all_to_all | solution.py:41
  53.2 0.0 copy-done.3
  53.3 1.1 %project.1 = bf16[32,64,256]{2,1,0:T(8,128)(2,1)S(1)} custom-call(bf16[32,72,128]{2,1,0:T(8,128)(2,1)S(1)} %all_to_all.25.got, f32[64,128]{1,0:T(8,128)S(1)} %get-tuple-element.11.o_tree, f32[8,64]{1,0:T(8,128)S(1)} %get-tuple-element.12.lse_tree, bf16[128,8192]{1,0:T(8,128)(2,1)S(1)} %copy-done.3), custom_call_target="tpu_custom_call" | custom-call | tf_op jit(solution)/shard_map/project/pallas_call | solution.py:271
  54.3 0.0 copy-start.8
  54.3 12.5 %all_to_all.26 = bf16[4,512,256]{2,1,0:T(8,128)(2,1)S(1)} all-to-all(bf16[4,512,256]{2,1,0:T(8,128)(2,1)S(1)} %bitcast.5), channel_id=1, replica_groups={{0,8,16,24},{1,9,17,25},{2,10,18,26},{3,11,19,27},{4,12,20,28},{5,13,21..., dimensions={0} | all-to-all | bytes 2097152 | tf_op jit(solution)/shard_map/all_to_all | solution.py:54
  66.8 0.1 join.1
  67.0 12.8 %all_to_all.27.got = bf16[8,64,256]{2,1,0:T(8,128)(2,1)S(1)} all-to-all(bf16[8,64,256]{2,1,0:T(8,128)(2,1)S(1)} %join.1), channel_id=1, replica_groups={{0,1,2,3,4,5,6,7},{8,9,10,11,12,13,14,15},{16,17,18,19,20,21,22,23},{24..., dimensions={0} | all-to-all | bytes 524288 | tf_op jit(solution)/shard_map/all_to_all | solution.py:54
  79.8 0.0 copy-done.8
  79.8 0.7 hidden.1
  80.4 11.8 %all_to_all.28.got = bf16[32,8,128]{2,1,0:T(8,128)(2,1)S(1)} all-to-all(bf16[32,8,128]{2,1,0:T(8,128)(2,1)S(1)} %get-tuple-element.14), channel_id=1, replica_groups=mesh['dp'=16,'tensor'=32] {'tensor'}, dimensions={0} | all-to-all | bytes 131072 | tf_op jit(solution)/shard_map/all_to_all | solution.py:41
  92.3 0.9 draft.1
Async XLA Ops:
  0.6 22.6 %copy-start = (bf16[4,256,512]{2,1,0:T(8,128)(2,1)S(1)}, bf16[4,256,512]{2,1,0:T(8,128)(2,1)}, u32[]{:S(2)}) copy-start(bf16[4,256,512]{2,1,0:T(8,128)(2,1)} %k.3) | copy-start | bytes 3145732
  0.7 0.8 copy-start.4
  12.1 21.9 %all-to-all-start = ((bf16[32,64,128]{2,1,0:T(8,128)(2,1)}), bf16[32,64,128]{2,1,0:T(8,128)(2,1)S(1)}, u32[]{:S(2)}, u32[]{:S(2)}) async-start(bf16[32,64,128]{2,1,0:T(8,128)(2,1)} %spread.1), calls=%async_computation | async-start | bytes 1048576 | tf_op jit(solution)/shard_map/all_to_all | solution.py:41
  23.3 1.2 %copy-start.1 = (bf16[4,256,512]{2,1,0:T(8,128)(2,1)S(1)}, bf16[4,256,512]{2,1,0:T(8,128)(2,1)}, u32[]{:S(2)}) copy-start(bf16[4,256,512]{2,1,0:T(8,128)(2,1)} %v.3) | copy-start | bytes 3145732
  24.5 0.7 copy-start.5
  25.2 0.8 copy-start.6
  26.1 0.8 copy-start.7
  26.9 0.7 copy-start.9
  27.6 0.7 copy-start.10
  28.2 0.7 copy-start.11
  28.9 5.1 %copy-start.2 = (bf16[4,256,512]{2,1,0:T(8,128)(2,1)S(1)}, bf16[4,256,512]{2,1,0:T(8,128)(2,1)}, u32[]{:S(2)}) copy-start(bf16[4,256,512]{2,1,0:T(8,128)(2,1)} %v.3) | copy-start | bytes 3145732
  34.0 19.3 %copy-start.3 = (bf16[128,8192]{1,0:T(8,128)(2,1)S(1)}, bf16[128,8192]{1,0:T(8,128)(2,1)}, u32[]{:S(2)}) copy-start(bf16[128,8192]{1,0:T(8,128)(2,1)} %wo.1) | copy-start | bytes 6291460
  54.3 25.4 %copy-start.8 = (bf16[64,256]{1,0:T(8,128)(2,1)S(1)}, bf16[64,256]{1,0:T(8,128)(2,1)}, u32[]{:S(2)}) copy-start(bf16[64,256]{1,0:T(8,128)(2,1)} %residual.1) | copy-start | bytes 98308

commit v5 on v4

--- a/solution.py
+++ b/solution.py
@@ -24,7 +24,7 @@
 bf16 = jnp.bfloat16
 VM = pl.BlockSpec(memory_space=pltpu.VMEM)
 SM = pl.BlockSpec(memory_space=pltpu.SMEM)
-STAGGER = 9800
+STAGGER = 9400
 
 
 def iota(shape, dim):
@@ -166,7 +166,8 @@
     width = out.shape[2]
     for d in range(out.shape[0]):
         part = jnp.dot(att, wo[:, d * width : (d + 1) * width], preferred_element_type=f32)
-        out[d] = part.astype(bf16)
+        x, y = d // 8, d % 8
+        out[x * 8 + (y % 2) * 4 + y // 2] = part.astype(bf16)
 
 
 def join_kernel(got, out):
@@ -276,19 +277,18 @@
         in_specs=[VM, VM, VM, VM],
         out_specs=VM,
     )(got, o_tree, lse_tree, wo_rows)
-    lines, size = 4, count // 4
-    along_x = [[x * size + y for x in range(lines)] for y in range(size)]
-    along_y = [[x * size + y for y in range(size)] for x in range(lines)]
-    part = across(terms.reshape(lines, size * ROWS, width), along_x)
+    blocks = [[x * 8 + 2 * b + a for x in range(4) for a in range(2)] for b in range(4)]
+    strides = [[x * 8 + 2 * b + a for b in range(4)] for x in range(4) for a in range(2)]
+    part = across(terms.reshape(8, 4 * ROWS, width), blocks)
     joined = pl.pallas_call(
         join_kernel,
         name="join",
         compiler_params=params(6),
-        out_shape=shape((size, ROWS, width), bf16),
+        out_shape=shape((4, ROWS, width), bf16),
         in_specs=[VM],
         out_specs=VM,
-    )(part.reshape(lines, size, ROWS, width))
-    arrived = across(joined, along_y)
+    )(part.reshape(8, 4, ROWS, width))
+    arrived = across(joined, strides)
     h, layer_out, squares = pl.pallas_call(
         hidden_kernel,
         name="hidden",

time: 93.8 us -> 93 us (level)
    all_to_all x2, blocking collectives: 25.3 us -> 23.5 us  [across(): lax.all_to_all(x, 'tensor', split_axis=0, concat_axis=0, axis_index_group...]
    all_to_all x2, blocking collectives: 29.4 us -> 30.8 us  [to_all(): return lax.all_to_all(x, 'tensor', split_axis=0, concat_axis=0, tiled=True)]
where the time goes in v5:
time: 93 us; the launch traced here: 92.3 us
  blocking collectives  54.3 us (58%)
  Pallas kernels  16 us (17%)
  starting transfers between devices  10.5 us (11%)
  local copies, waits for them, and re-layouts  7.09 us (8%)
  waiting for transfers between devices  3.77 us (4%)
    all_to_all x2, blocking collectives, to_all(): return lax.all_to_all(x, 'tensor', split_axis=0, concat_axis=0, tiled=True)  30.8 us
    all_to_all x2, blocking collectives, across(): lax.all_to_all(x, 'tensor', split_axis=0, concat_axis=0, axis_index_group...  23.5 us
    all_to_all x1, starting transfers between devices, to_all(): return lax.all_to_all(x, 'tensor', split_axis=0, concat_axis=0, tiled=True)  10.5 us
    pallas_call x1, Pallas kernels, on_device(): pl.pallas_call(spread_kernel, name='spread', compiler_params=params(2), o...  10.3 us
    unnamed x24, local copies, waits for them, and re-layouts  6.43 us
    all_to_all x1, waiting for transfers between devices, to_all(): return lax.all_to_all(x, 'tensor', split_axis=0, concat_axis=0, tiled=True)  3.77 us
  transfers between devices with their start and end apart: 1, of which 1 were waited for; matrix products, arithmetic and copies ran while one was open for 1% of the time, Pallas kernels for 1%

profile of v5, /device:TPU:1, one launch (start us, length us, event | category | flops | bytes accessed | tf_op | source)
XLA Modules:
  0.0 92.3 jit_solution(17206004486369435076)
XLA Ops:
  0.6 0.0 copy-start
  0.7 0.0 copy-start.4
  0.7 0.8 copy-done.4
  1.5 10.3 %spread.1 = bf16[32,64,128]{2,1,0:T(8,128)(2,1)} custom-call(s32[1]{0:T(128)S(6)} %select_n.7.late, bf16[64,128]{1,0:T(8,128)(2,1)S(1)} %copy-done.4), custom_call_target="tpu_custom_call" | custom-call | tf_op jit(solution)/shard_map/spread/pallas_call | solution.py:236
  11.7 10.5 %all-to-all-start = ((bf16[32,64,128]{2,1,0:T(8,128)(2,1)}), bf16[32,64,128]{2,1,0:T(8,128)(2,1)S(1)}, u32[]{:S(2)}, u32[]{:S(2)}) async-start(bf16[32,64,128]{2,1,0:T(8,128)(2,1)} %spread.1), calls=%async_computation | async-start | bytes 1048576 | tf_op jit(solution)/shard_map/all_to_all | solution.py:41
  22.2 0.7 reshape.25.gain
  22.9 0.0 copy-done
  22.9 0.0 copy-start.1
  22.9 1.2 %copy-done.1 = bf16[4,256,512]{2,1,0:T(8,128)(2,1)S(1)} copy-done((bf16[4,256,512]{2,1,0:T(8,128)(2,1)S(1)}, bf16[4,256,512]{2,1,0:T(8,128)(2,1)}, u32[]{:S(2)}) %copy-start.1) | copy-done | bytes 1048600
  24.1 0.0 copy-start.5
  24.1 0.7 copy-done.5
  24.8 0.0 copy-start.6
  24.8 0.8 copy-done.6
  25.7 0.0 copy-start.7
  25.7 0.8 copy-done.7
  26.5 0.0 copy-start.9
  26.5 0.7 copy-done.9
  27.2 0.0 copy-start.10
  27.2 0.7 copy-done.10
  27.8 0.0 copy-start.11
  27.8 0.7 copy-done.11
  28.5 0.0 copy-start.2
  28.5 1.3 %tree.1 = (f32[64,128]{1,0:T(8,128)S(1)}, f32[8,64]{1,0:T(8,128)S(1)}, bf16[32,64]{1,0:T(8,128)(2,1)S(1)}, s32[4,8,128]{2,1,0:T(8,128)S(1)}, f32[8,256]{1,0:T(8,128)S(1)}) custom-call(s32[1]{0:T(128)} %bitcast.rank, s32[4,16]{1,0:T(4,128)S(1)} %copy-done.9, s32[4]{0:T(128)S(1)} %copy-done.10, s32[4]{0:T(128)S(1)} %copy-done.11, ...), custom_call_target="tpu_custom_call" | custom-call | flops 100000000 | bytes 4000000 | tf_op jit(solution)/shard_map/tree/pallas_call | solution.py:245
  29.8 3.8 %all-to-all-done.q = bf16[32,64,128]{2,1,0:T(8,128)(2,1)S(1)} async-done(((bf16[32,64,128]{2,1,0:T(8,128)(2,1)}), bf16[32,64,128]{2,1,0:T(8,128)(2,1)S(1)}, u32[]{:S(2)}, u32[]{:S(2)}) %all-to-all-start) | async-done | bytes 524320 | tf_op jit(solution)/shard_map/all_to_all | solution.py:41
  33.6 0.0 copy-done.2
  33.6 0.0 copy-start.3
  33.6 1.7 %attend.1 = bf16[32,72,128]{2,1,0:T(8,128)(2,1)S(1)} custom-call(s32[4,8,128]{2,1,0:T(8,128)S(1)} %get-tuple-element.10.left, bf16[32,64,128]{2,1,0:T(8,128)(2,1)S(1)} %all-to-all-done.q, bf16[4,256,512]{2,1,0:T(8,128)(2,1)S(1)} %copy-done, bf16[4,256,512]{2,1,0:T(8,128)(2,1)S(1)} %copy-done.2), custom_call_target="tpu_custom_call" | custom-call | tf_op jit(solution)/shard_map/attend/pallas_call | solution.py:263
  35.3 18.9 %all_to_all.25.got = bf16[32,72,128]{2,1,0:T(8,128)(2,1)S(1)} all-to-all(bf16[32,72,128]{2,1,0:T(8,128)(2,1)S(1)} %attend.1), channel_id=1, replica_groups=mesh['dp'=16,'tensor'=32] {'tensor'}, dimensions={0} | all-to-all | bytes 1179648 | tf_op jit(solution)/shard_map/all_to_all | solution.py:41
  54.2 0.0 copy-done.3
  54.2 1.1 %project.1 = bf16[32,64,256]{2,1,0:T(8,128)(2,1)S(1)} custom-call(bf16[32,72,128]{2,1,0:T(8,128)(2,1)S(1)} %all_to_all.25.got, f32[64,128]{1,0:T(8,128)S(1)} %get-tuple-element.11.o_tree, f32[8,64]{1,0:T(8,128)S(1)} %get-tuple-element.12.lse_tree, bf16[128,8192]{1,0:T(8,128)(2,1)S(1)} %copy-done.3), custom_call_target="tpu_custom_call" | custom-call | tf_op jit(solution)/shard_map/project/pallas_call | solution.py:272
  55.3 0.0 copy-start.8
  55.3 13.9 %all_to_all.26 = bf16[8,256,256]{2,1,0:T(8,128)(2,1)S(1)} all-to-all(bf16[8,256,256]{2,1,0:T(8,128)(2,1)S(1)} %bitcast.5), channel_id=1, replica_groups={{0,1,8,9,16,17,24,25},{2,3,10,11,18,19,26,27},{4,5,12,13,20,21,28,29},{..., dimensions={0} | all-to-all | bytes 2097152 | tf_op jit(solution)/shard_map/all_to_all | solution.py:54
  69.2 0.1 join.1
  69.3 9.6 %all_to_all.27.got = bf16[4,64,256]{2,1,0:T(8,128)(2,1)S(1)} all-to-all(bf16[4,64,256]{2,1,0:T(8,128)(2,1)S(1)} %join.1), channel_id=1, replica_groups={{0,2,4,6},{1,3,5,7},{8,10,12,14},{9,11,13,15},{16,18,20,22},{17,19,21,2..., dimensions={0} | all-to-all | bytes 262144 | tf_op jit(solution)/shard_map/all_to_all | solution.py:54
  78.9 0.0 copy-done.8
  78.9 0.6 hidden.1
  79.6 11.9 %all_to_all.28.got = bf16[32,8,128]{2,1,0:T(8,128)(2,1)S(1)} all-to-all(bf16[32,8,128]{2,1,0:T(8,128)(2,1)S(1)} %get-tuple-element.14), channel_id=1, replica_groups=mesh['dp'=16,'tensor'=32] {'tensor'}, dimensions={0} | all-to-all | bytes 131072 | tf_op jit(solution)/shard_map/all_to_all | solution.py:41
  91.5 0.9 draft.1
Async XLA Ops:
  0.6 22.2 %copy-start = (bf16[4,256,512]{2,1,0:T(8,128)(2,1)S(1)}, bf16[4,256,512]{2,1,0:T(8,128)(2,1)}, u32[]{:S(2)}) copy-start(bf16[4,256,512]{2,1,0:T(8,128)(2,1)} %k.3) | copy-start | bytes 3145732
  0.7 0.8 copy-start.4
  11.7 21.9 %all-to-all-start = ((bf16[32,64,128]{2,1,0:T(8,128)(2,1)}), bf16[32,64,128]{2,1,0:T(8,128)(2,1)S(1)}, u32[]{:S(2)}, u32[]{:S(2)}) async-start(bf16[32,64,128]{2,1,0:T(8,128)(2,1)} %spread.1), calls=%async_computation | async-start | bytes 1048576 | tf_op jit(solution)/shard_map/all_to_all | solution.py:41
  22.9 1.2 %copy-start.1 = (bf16[4,256,512]{2,1,0:T(8,128)(2,1)S(1)}, bf16[4,256,512]{2,1,0:T(8,128)(2,1)}, u32[]{:S(2)}) copy-start(bf16[4,256,512]{2,1,0:T(8,128)(2,1)} %v.3) | copy-start | bytes 3145732
  24.1 0.7 copy-start.5
  24.8 0.8 copy-start.6
  25.7 0.8 copy-start.7
  26.5 0.7 copy-start.9
  27.2 0.7 copy-start.10
  27.8 0.7 copy-start.11
  28.5 5.1 %copy-start.2 = (bf16[4,256,512]{2,1,0:T(8,128)(2,1)S(1)}, bf16[4,256,512]{2,1,0:T(8,128)(2,1)}, u32[]{:S(2)}) copy-start(bf16[4,256,512]{2,1,0:T(8,128)(2,1)} %v.3) | copy-start | bytes 3145732
  33.6 20.6 %copy-start.3 = (bf16[128,8192]{1,0:T(8,128)(2,1)S(1)}, bf16[128,8192]{1,0:T(8,128)(2,1)}, u32[]{:S(2)}) copy-start(bf16[128,8192]{1,0:T(8,128)(2,1)} %wo.1) | copy-start | bytes 6291460
  55.3 23.7 %copy-start.8 = (bf16[64,256]{1,0:T(8,128)(2,1)S(1)}, bf16[64,256]{1,0:T(8,128)(2,1)}, u32[]{:S(2)}) copy-start(bf16[64,256]{1,0:T(8,128)(2,1)} %residual.1) | copy-start | bytes 98308

commit v6 on v5

--- a/solution.py
+++ b/solution.py
@@ -24,7 +24,7 @@
 bf16 = jnp.bfloat16
 VM = pl.BlockSpec(memory_space=pltpu.VMEM)
 SM = pl.BlockSpec(memory_space=pltpu.SMEM)
-STAGGER = 9400
+STAGGER = 9600
 
 
 def iota(shape, dim):
@@ -178,12 +178,11 @@
         out[d] = total.astype(bf16)
 
 
-def hidden_kernel(got, residual, h_ref, layer_ref, sq_ref):
+def hidden_kernel(got, residual, h_ref, sq_ref):
     h = residual[...].astype(f32)
     for c in range(got.shape[0]):
         h = h + got[c].astype(f32)
     h_ref[...] = h
-    layer_ref[...] = h.astype(bf16)
     sq = h * h
     part = sq[:, :HD]
     for c in range(HD, sq.shape[1], HD):
@@ -197,7 +196,8 @@
         sq_ref[c] = tile
 
 
-def draft_kernel(got, h, gain, sel, out):
+def draft_kernel(got, h, gain, sel, out, layer_ref):
+    layer_ref[...] = h[...].astype(bf16)
     tile = got[0].astype(f32)
     for c in range(1, got.shape[0]):
         tile = tile + got[c].astype(f32)
@@ -289,22 +289,22 @@
         out_specs=VM,
     )(part.reshape(8, 4, ROWS, width))
     arrived = across(joined, strides)
-    h, layer_out, squares = pl.pallas_call(
+    h, squares = pl.pallas_call(
         hidden_kernel,
         name="hidden",
         compiler_params=params(6),
-        out_shape=(shape((ROWS, width), f32), shape((ROWS, width), bf16), shape((count, STAT, HD), bf16)),
+        out_shape=(shape((ROWS, width), f32), shape((count, STAT, HD), bf16)),
         in_specs=[VM, VM],
-        out_specs=(VM, VM, VM),
+        out_specs=(VM, VM),
     )(arrived, residual)
     totals = to_all(squares)
-    draft = pl.pallas_call(
+    draft, layer_out = pl.pallas_call(
         draft_kernel,
         name="draft",
         compiler_params=params(4),
-        out_shape=shape((REQ * MAXACC, width), bf16),
+        out_shape=(shape((REQ * MAXACC, width), bf16), shape((ROWS, width), bf16)),
         in_specs=[VM, VM, VM, VM],
-        out_specs=VM,
+        out_specs=(VM, VM),
     )(totals, h, gains, sel)
     return (layer_out, draft.reshape(REQ, MAXACC, width))
 

time: 93 us -> 92.4 us (level)
  no operation moved by 1% of the time
where the time goes in v6:
time: 92.4 us; the launch traced here: 91.7 us
  blocking collectives  54 us (58%)
  Pallas kernels  15.7 us (17%)
  starting transfers between devices  10.5 us (11%)
  local copies, waits for them, and re-layouts  7.09 us (8%)
  waiting for transfers between devices  3.77 us (4%)
    all_to_all x2, blocking collectives, to_all(): return lax.all_to_all(x, 'tensor', split_axis=0, concat_axis=0, tiled=True)  30.3 us
    all_to_all x2, blocking collectives, across(): lax.all_to_all(x, 'tensor', split_axis=0, concat_axis=0, axis_index_group...  23.7 us
    all_to_all x1, starting transfers between devices, to_all(): return lax.all_to_all(x, 'tensor', split_axis=0, concat_axis=0, tiled=True)  10.5 us
    pallas_call x1, Pallas kernels, on_device(): pl.pallas_call(spread_kernel, name='spread', compiler_params=params(2), o...  10.5 us
    unnamed x24, local copies, waits for them, and re-layouts  6.43 us
    all_to_all x1, waiting for transfers between devices, to_all(): return lax.all_to_all(x, 'tensor', split_axis=0, concat_axis=0, tiled=True)  3.77 us
  transfers between devices with their start and end apart: 1, of which 1 were waited for; matrix products, arithmetic and copies ran while one was open for 1% of the time, Pallas kernels for 1%

profile of v6, /device:TPU:1, one launch (start us, length us, event | category | flops | bytes accessed | tf_op | source)
XLA Modules:
  0.0 91.7 jit_solution(5943486482029219381)
XLA Ops:
  0.6 0.0 copy-start
  0.7 0.0 copy-start.4
  0.7 0.8 copy-done.4
  1.5 10.5 %spread.1 = bf16[32,64,128]{2,1,0:T(8,128)(2,1)} custom-call(s32[1]{0:T(128)S(6)} %select_n.7.late, bf16[64,128]{1,0:T(8,128)(2,1)S(1)} %copy-done.4), custom_call_target="tpu_custom_call" | custom-call | tf_op jit(solution)/shard_map/spread/pallas_call | solution.py:236
  11.9 10.5 %all-to-all-start = ((bf16[32,64,128]{2,1,0:T(8,128)(2,1)}), bf16[32,64,128]{2,1,0:T(8,128)(2,1)S(1)}, u32[]{:S(2)}, u32[]{:S(2)}) async-start(bf16[32,64,128]{2,1,0:T(8,128)(2,1)} %spread.1), calls=%async_computation | async-start | bytes 1048576 | tf_op jit(solution)/shard_map/all_to_all | solution.py:41
  22.4 0.7 reshape.25.gain
  23.1 0.0 copy-done
  23.1 0.0 copy-start.1
  23.1 1.2 %copy-done.1 = bf16[4,256,512]{2,1,0:T(8,128)(2,1)S(1)} copy-done((bf16[4,256,512]{2,1,0:T(8,128)(2,1)S(1)}, bf16[4,256,512]{2,1,0:T(8,128)(2,1)}, u32[]{:S(2)}) %copy-start.1) | copy-done | bytes 1048600
  24.3 0.0 copy-start.5
  24.3 0.7 copy-done.5
  25.0 0.0 copy-start.6
  25.0 0.8 copy-done.6
  25.9 0.0 copy-start.7
  25.9 0.8 copy-done.7
  26.7 0.0 copy-start.9
  26.7 0.7 copy-done.9
  27.4 0.0 copy-start.10
  27.4 0.7 copy-done.10
  28.0 0.0 copy-start.11
  28.0 0.7 copy-done.11
  28.7 0.0 copy-start.2
  28.7 1.3 %tree.1 = (f32[64,128]{1,0:T(8,128)S(1)}, f32[8,64]{1,0:T(8,128)S(1)}, bf16[32,64]{1,0:T(8,128)(2,1)S(1)}, s32[4,8,128]{2,1,0:T(8,128)S(1)}, f32[8,256]{1,0:T(8,128)S(1)}) custom-call(s32[1]{0:T(128)} %bitcast.rank, s32[4,16]{1,0:T(4,128)S(1)} %copy-done.9, s32[4]{0:T(128)S(1)} %copy-done.10, s32[4]{0:T(128)S(1)} %copy-done.11, ...), custom_call_target="tpu_custom_call" | custom-call | flops 100000000 | bytes 4000000 | tf_op jit(solution)/shard_map/tree/pallas_call | solution.py:245
  30.0 3.8 %all-to-all-done.q = bf16[32,64,128]{2,1,0:T(8,128)(2,1)S(1)} async-done(((bf16[32,64,128]{2,1,0:T(8,128)(2,1)}), bf16[32,64,128]{2,1,0:T(8,128)(2,1)S(1)}, u32[]{:S(2)}, u32[]{:S(2)}) %all-to-all-start) | async-done | bytes 524320 | tf_op jit(solution)/shard_map/all_to_all | solution.py:41
  33.8 0.0 copy-done.2
  33.8 0.0 copy-start.3
  33.8 1.7 %attend.1 = bf16[32,72,128]{2,1,0:T(8,128)(2,1)S(1)} custom-call(s32[4,8,128]{2,1,0:T(8,128)S(1)} %get-tuple-element.11.left, bf16[32,64,128]{2,1,0:T(8,128)(2,1)S(1)} %all-to-all-done.q, bf16[4,256,512]{2,1,0:T(8,128)(2,1)S(1)} %copy-done, bf16[4,256,512]{2,1,0:T(8,128)(2,1)S(1)} %copy-done.2), custom_call_target="tpu_custom_call" | custom-call | tf_op jit(solution)/shard_map/attend/pallas_call | solution.py:263
  35.5 18.5 %all_to_all.25.got = bf16[32,72,128]{2,1,0:T(8,128)(2,1)S(1)} all-to-all(bf16[32,72,128]{2,1,0:T(8,128)(2,1)S(1)} %attend.1), channel_id=1, replica_groups=mesh['dp'=16,'tensor'=32] {'tensor'}, dimensions={0} | all-to-all | bytes 1179648 | tf_op jit(solution)/shard_map/all_to_all | solution.py:41
  53.9 0.0 copy-done.3
  53.9 1.1 %project.1 = bf16[32,64,256]{2,1,0:T(8,128)(2,1)S(1)} custom-call(bf16[32,72,128]{2,1,0:T(8,128)(2,1)S(1)} %all_to_all.25.got, f32[64,128]{1,0:T(8,128)S(1)} %get-tuple-element.12.o_tree, f32[8,64]{1,0:T(8,128)S(1)} %get-tuple-element.13.lse_tree, bf16[128,8192]{1,0:T(8,128)(2,1)S(1)} %copy-done.3), custom_call_target="tpu_custom_call" | custom-call | tf_op jit(solution)/shard_map/project/pallas_call | solution.py:272
  55.0 0.0 copy-start.8
  55.0 14.1 %all_to_all.26 = bf16[8,256,256]{2,1,0:T(8,128)(2,1)S(1)} all-to-all(bf16[8,256,256]{2,1,0:T(8,128)(2,1)S(1)} %bitcast.5), channel_id=1, replica_groups={{0,1,8,9,16,17,24,25},{2,3,10,11,18,19,26,27},{4,5,12,13,20,21,28,29},{..., dimensions={0} | all-to-all | bytes 2097152 | tf_op jit(solution)/shard_map/all_to_all | solution.py:54
  69.1 0.1 join.1
  69.3 9.6 %all_to_all.27.got = bf16[4,64,256]{2,1,0:T(8,128)(2,1)S(1)} all-to-all(bf16[4,64,256]{2,1,0:T(8,128)(2,1)S(1)} %join.1), channel_id=1, replica_groups={{0,2,4,6},{1,3,5,7},{8,10,12,14},{9,11,13,15},{16,18,20,22},{17,19,21,2..., dimensions={0} | all-to-all | bytes 262144 | tf_op jit(solution)/shard_map/all_to_all | solution.py:54
  78.9 0.0 copy-done.8
  78.9 0.1 hidden.1
  79.0 11.9 %all_to_all.28.got = bf16[32,8,128]{2,1,0:T(8,128)(2,1)S(1)} all-to-all(bf16[32,8,128]{2,1,0:T(8,128)(2,1)S(1)} %get-tuple-element.14), channel_id=1, replica_groups=mesh['dp'=16,'tensor'=32] {'tensor'}, dimensions={0} | all-to-all | bytes 131072 | tf_op jit(solution)/shard_map/all_to_all | solution.py:41
  90.9 0.9 draft.1
Async XLA Ops:
  0.6 22.5 %copy-start = (bf16[4,256,512]{2,1,0:T(8,128)(2,1)S(1)}, bf16[4,256,512]{2,1,0:T(8,128)(2,1)}, u32[]{:S(2)}) copy-start(bf16[4,256,512]{2,1,0:T(8,128)(2,1)} %k.3) | copy-start | bytes 3145732
  0.7 0.8 copy-start.4
  11.9 21.9 %all-to-all-start = ((bf16[32,64,128]{2,1,0:T(8,128)(2,1)}), bf16[32,64,128]{2,1,0:T(8,128)(2,1)S(1)}, u32[]{:S(2)}, u32[]{:S(2)}) async-start(bf16[32,64,128]{2,1,0:T(8,128)(2,1)} %spread.1), calls=%async_computation | async-start | bytes 1048576 | tf_op jit(solution)/shard_map/all_to_all | solution.py:41
  23.1 1.2 %copy-start.1 = (bf16[4,256,512]{2,1,0:T(8,128)(2,1)S(1)}, bf16[4,256,512]{2,1,0:T(8,128)(2,1)}, u32[]{:S(2)}) copy-start(bf16[4,256,512]{2,1,0:T(8,128)(2,1)} %v.3) | copy-start | bytes 3145732
  24.3 0.7 copy-start.5
  25.0 0.8 copy-start.6
  25.9 0.8 copy-start.7
  26.7 0.7 copy-start.9
  27.4 0.7 copy-start.10
  28.0 0.7 copy-start.11
  28.7 5.1 %copy-start.2 = (bf16[4,256,512]{2,1,0:T(8,128)(2,1)S(1)}, bf16[4,256,512]{2,1,0:T(8,128)(2,1)}, u32[]{:S(2)}) copy-start(bf16[4,256,512]{2,1,0:T(8,128)(2,1)} %v.3) | copy-start | bytes 3145732
  33.8 20.1 %copy-start.3 = (bf16[128,8192]{1,0:T(8,128)(2,1)S(1)}, bf16[128,8192]{1,0:T(8,128)(2,1)}, u32[]{:S(2)}) copy-start(bf16[128,8192]{1,0:T(8,128)(2,1)} %wo.1) | copy-start | bytes 6291460
  55.0 23.9 %copy-start.8 = (bf16[64,256]{1,0:T(8,128)(2,1)S(1)}, bf16[64,256]{1,0:T(8,128)(2,1)}, u32[]{:S(2)}) copy-start(bf16[64,256]{1,0:T(8,128)(2,1)} %residual.1) | copy-start | bytes 98308

commit v7 on v6

--- a/solution.py
+++ b/solution.py
@@ -110,10 +110,10 @@
     sub = iota((GROUP, HD), 0)
     lane = iota((GROUP, HD), 1)
     packed = [jnp.zeros((GROUP, HD), f32)] * KVH
-    for r in range(REQ):
-        rows = slice(r * TREE, (r + 1) * TREE)
-        valid = pos < left[r, 0:1, :]
-        for g in range(KVH):
+    for g in range(KVH):
+        for r in range(REQ):
+            rows = slice(r * TREE, (r + 1) * TREE)
+            valid = pos < left[r, 0:1, :]
             cols = slice(g * HD, (g + 1) * HD)
             heads = slice(g * GROUP, (g + 1) * GROUP)
             qh = q[heads, rows, :].reshape(GROUP * TREE, HD)

time: 92.4 us -> 92.4 us (level)
  no operation moved by 1% of the time
where the time goes in v7:
time: 92.4 us; the launch traced here: 91.7 us
  blocking collectives  54 us (58%)
  Pallas kernels  15.7 us (17%)
  starting transfers between devices  10.5 us (11%)
  local copies, waits for them, and re-layouts  7.09 us (8%)
  waiting for transfers between devices  3.77 us (4%)
    all_to_all x2, blocking collectives, to_all(): return lax.all_to_all(x, 'tensor', split_axis=0, concat_axis=0, tiled=True)  30.3 us
    all_to_all x2, blocking collectives, across(): lax.all_to_all(x, 'tensor', split_axis=0, concat_axis=0, axis_index_group...  23.7 us
    all_to_all x1, starting transfers between devices, to_all(): return lax.all_to_all(x, 'tensor', split_axis=0, concat_axis=0, tiled=True)  10.5 us
    pallas_call x1, Pallas kernels, on_device(): pl.pallas_call(spread_kernel, name='spread', compiler_params=params(2), o...  10.5 us
    unnamed x24, local copies, waits for them, and re-layouts  6.43 us
    all_to_all x1, waiting for transfers between devices, to_all(): return lax.all_to_all(x, 'tensor', split_axis=0, concat_axis=0, tiled=True)  3.77 us
  transfers between devices with their start and end apart: 1, of which 1 were waited for; matrix products, arithmetic and copies ran while one was open for 1% of the time, Pallas kernels for 1%

profile of v7, /device:TPU:1, one launch (start us, length us, event | category | flops | bytes accessed | tf_op | source)
XLA Modules:
  0.0 91.7 jit_solution(9985312748203431245)
XLA Ops:
  0.6 0.0 copy-start
  0.7 0.0 copy-start.4
  0.7 0.8 copy-done.4
  1.5 10.5 %spread.1 = bf16[32,64,128]{2,1,0:T(8,128)(2,1)} custom-call(s32[1]{0:T(128)S(6)} %select_n.7.late, bf16[64,128]{1,0:T(8,128)(2,1)S(1)} %copy-done.4), custom_call_target="tpu_custom_call" | custom-call | tf_op jit(solution)/shard_map/spread/pallas_call | solution.py:236
  11.9 10.5 %all-to-all-start = ((bf16[32,64,128]{2,1,0:T(8,128)(2,1)}), bf16[32,64,128]{2,1,0:T(8,128)(2,1)S(1)}, u32[]{:S(2)}, u32[]{:S(2)}) async-start(bf16[32,64,128]{2,1,0:T(8,128)(2,1)} %spread.1), calls=%async_computation | async-start | bytes 1048576 | tf_op jit(solution)/shard_map/all_to_all | solution.py:41
  22.4 0.7 reshape.25.gain
  23.1 0.0 copy-done
  23.1 0.0 copy-start.1
  23.1 1.2 %copy-done.1 = bf16[4,256,512]{2,1,0:T(8,128)(2,1)S(1)} copy-done((bf16[4,256,512]{2,1,0:T(8,128)(2,1)S(1)}, bf16[4,256,512]{2,1,0:T(8,128)(2,1)}, u32[]{:S(2)}) %copy-start.1) | copy-done | bytes 1048600
  24.3 0.0 copy-start.5
  24.3 0.7 copy-done.5
  25.0 0.0 copy-start.6
  25.0 0.8 copy-done.6
  25.9 0.0 copy-start.7
  25.9 0.8 copy-done.7
  26.7 0.0 copy-start.9
  26.7 0.7 copy-done.9
  27.4 0.0 copy-start.10
  27.4 0.7 copy-done.10
  28.0 0.0 copy-start.11
  28.0 0.7 copy-done.11
  28.7 0.0 copy-start.2
  28.7 1.3 %tree.1 = (f32[64,128]{1,0:T(8,128)S(1)}, f32[8,64]{1,0:T(8,128)S(1)}, bf16[32,64]{1,0:T(8,128)(2,1)S(1)}, s32[4,8,128]{2,1,0:T(8,128)S(1)}, f32[8,256]{1,0:T(8,128)S(1)}) custom-call(s32[1]{0:T(128)} %bitcast.rank, s32[4,16]{1,0:T(4,128)S(1)} %copy-done.9, s32[4]{0:T(128)S(1)} %copy-done.10, s32[4]{0:T(128)S(1)} %copy-done.11, ...), custom_call_target="tpu_custom_call" | custom-call | flops 100000000 | bytes 4000000 | tf_op jit(solution)/shard_map/tree/pallas_call | solution.py:245
  30.0 3.8 %all-to-all-done.q = bf16[32,64,128]{2,1,0:T(8,128)(2,1)S(1)} async-done(((bf16[32,64,128]{2,1,0:T(8,128)(2,1)}), bf16[32,64,128]{2,1,0:T(8,128)(2,1)S(1)}, u32[]{:S(2)}, u32[]{:S(2)}) %all-to-all-start) | async-done | bytes 524320 | tf_op jit(solution)/shard_map/all_to_all | solution.py:41
  33.8 0.0 copy-done.2
  33.8 0.0 copy-start.3
  33.8 1.7 %attend.1 = bf16[32,72,128]{2,1,0:T(8,128)(2,1)S(1)} custom-call(s32[4,8,128]{2,1,0:T(8,128)S(1)} %get-tuple-element.11.left, bf16[32,64,128]{2,1,0:T(8,128)(2,1)S(1)} %all-to-all-done.q, bf16[4,256,512]{2,1,0:T(8,128)(2,1)S(1)} %copy-done, bf16[4,256,512]{2,1,0:T(8,128)(2,1)S(1)} %copy-done.2), custom_call_target="tpu_custom_call" | custom-call | tf_op jit(solution)/shard_map/attend/pallas_call | solution.py:263
  35.5 18.4 %all_to_all.25.got = bf16[32,72,128]{2,1,0:T(8,128)(2,1)S(1)} all-to-all(bf16[32,72,128]{2,1,0:T(8,128)(2,1)S(1)} %attend.1), channel_id=1, replica_groups=mesh['dp'=16,'tensor'=32] {'tensor'}, dimensions={0} | all-to-all | bytes 1179648 | tf_op jit(solution)/shard_map/all_to_all | solution.py:41
  53.9 0.0 copy-done.3
  53.9 1.1 %project.1 = bf16[32,64,256]{2,1,0:T(8,128)(2,1)S(1)} custom-call(bf16[32,72,128]{2,1,0:T(8,128)(2,1)S(1)} %all_to_all.25.got, f32[64,128]{1,0:T(8,128)S(1)} %get-tuple-element.12.o_tree, f32[8,64]{1,0:T(8,128)S(1)} %get-tuple-element.13.lse_tree, bf16[128,8192]{1,0:T(8,128)(2,1)S(1)} %copy-done.3), custom_call_target="tpu_custom_call" | custom-call | tf_op jit(solution)/shard_map/project/pallas_call | solution.py:272
  55.0 0.0 copy-start.8
  55.0 14.1 %all_to_all.26 = bf16[8,256,256]{2,1,0:T(8,128)(2,1)S(1)} all-to-all(bf16[8,256,256]{2,1,0:T(8,128)(2,1)S(1)} %bitcast.5), channel_id=1, replica_groups={{0,1,8,9,16,17,24,25},{2,3,10,11,18,19,26,27},{4,5,12,13,20,21,28,29},{..., dimensions={0} | all-to-all | bytes 2097152 | tf_op jit(solution)/shard_map/all_to_all | solution.py:54
  69.1 0.1 join.1
  69.3 9.6 %all_to_all.27.got = bf16[4,64,256]{2,1,0:T(8,128)(2,1)S(1)} all-to-all(bf16[4,64,256]{2,1,0:T(8,128)(2,1)S(1)} %join.1), channel_id=1, replica_groups={{0,2,4,6},{1,3,5,7},{8,10,12,14},{9,11,13,15},{16,18,20,22},{17,19,21,2..., dimensions={0} | all-to-all | bytes 262144 | tf_op jit(solution)/shard_map/all_to_all | solution.py:54
  78.9 0.0 copy-done.8
  78.9 0.1 hidden.1
  79.0 11.9 %all_to_all.28.got = bf16[32,8,128]{2,1,0:T(8,128)(2,1)S(1)} all-to-all(bf16[32,8,128]{2,1,0:T(8,128)(2,1)S(1)} %get-tuple-element.14), channel_id=1, replica_groups=mesh['dp'=16,'tensor'=32] {'tensor'}, dimensions={0} | all-to-all | bytes 131072 | tf_op jit(solution)/shard_map/all_to_all | solution.py:41
  90.9 0.9 draft.1
Async XLA Ops:
  0.6 22.5 %copy-start = (bf16[4,256,512]{2,1,0:T(8,128)(2,1)S(1)}, bf16[4,256,512]{2,1,0:T(8,128)(2,1)}, u32[]{:S(2)}) copy-start(bf16[4,256,512]{2,1,0:T(8,128)(2,1)} %k.3) | copy-start | bytes 3145732
  0.7 0.8 copy-start.4
  11.9 21.9 %all-to-all-start = ((bf16[32,64,128]{2,1,0:T(8,128)(2,1)}), bf16[32,64,128]{2,1,0:T(8,128)(2,1)S(1)}, u32[]{:S(2)}, u32[]{:S(2)}) async-start(bf16[32,64,128]{2,1,0:T(8,128)(2,1)} %spread.1), calls=%async_computation | async-start | bytes 1048576 | tf_op jit(solution)/shard_map/all_to_all | solution.py:41
  23.1 1.2 %copy-start.1 = (bf16[4,256,512]{2,1,0:T(8,128)(2,1)S(1)}, bf16[4,256,512]{2,1,0:T(8,128)(2,1)}, u32[]{:S(2)}) copy-start(bf16[4,256,512]{2,1,0:T(8,128)(2,1)} %v.3) | copy-start | bytes 3145732
  24.3 0.7 copy-start.5
  25.0 0.8 copy-start.6
  25.9 0.8 copy-start.7
  26.7 0.7 copy-start.9
  27.4 0.7 copy-start.10
  28.0 0.7 copy-start.11
  28.7 5.1 %copy-start.2 = (bf16[4,256,512]{2,1,0:T(8,128)(2,1)S(1)}, bf16[4,256,512]{2,1,0:T(8,128)(2,1)}, u32[]{:S(2)}) copy-start(bf16[4,256,512]{2,1,0:T(8,128)(2,1)} %v.3) | copy-start | bytes 3145732
  33.8 20.1 %copy-start.3 = (bf16[128,8192]{1,0:T(8,128)(2,1)S(1)}, bf16[128,8192]{1,0:T(8,128)(2,1)}, u32[]{:S(2)}) copy-start(bf16[128,8192]{1,0:T(8,128)(2,1)} %wo.1) | copy-start | bytes 6291460
  55.0 23.9 %copy-start.8 = (bf16[64,256]{1,0:T(8,128)(2,1)S(1)}, bf16[64,256]{1,0:T(8,128)(2,1)}, u32[]{:S(2)}) copy-start(bf16[64,256]{1,0:T(8,128)(2,1)} %residual.1) | copy-start | bytes 98308
